TPU v7x, 32 devices: a whole 2x2x4 slice. The times are simulated.
32 devices in a mesh: grp: 2 (over y), rows: 4 (over z), img: 2 (over x), tp: 2 (over core).
Axes of the slice: x: 2, y: 2, z: 4, core: 2. Of those that a mesh axis runs over, the one named last changes fastest.
Arguments:
- features: bfloat16 [16, 28, 2, 7168], P(('grp', 'img'), 'rows', 'tp'), parts along dimension 0, may hold values from -8 to 8
- gn_gain: float32 [128], P('tp'), may hold values from 0.5 to 1.5
- conv_w: bfloat16 [3, 3, 3, 128], P(None, None, None, 'tp'), may hold values from -0.1875 to 0.1875
- patch_w: bfloat16 [1280, 588], P('rows'), may hold values from -0.25 to 0.25
- pos_emb: bfloat16 [64, 1280], replicated, may hold values from -3 to 3
- ln1_gain: float32 [1280], replicated, may hold values from 0.5 to 1.5
- qkv_w: bfloat16 [1280, 3, 1280], P('rows', None, 'tp'), may hold values from -3 to 3
- out_w: bfloat16 [1280, 1280], P('rows', 'tp'), may hold values from -0.15625 to 0.15625
- final_gain: float32 [1280], replicated, may hold values from 0.5 to 1.5
- head_w: float32 [1280], replicated, may hold values from -0.15625 to 0.15625
- owner_slot: int32 [4, 4], P(('grp', 'img')), parts along dimension 0, may hold values from 0 to 3, each once within a row
Outputs:
- grad_features: bfloat16 [16, 28, 2, 7168], P(('grp', 'img'), 'rows', 'tp'), parts along dimension 0
- slot_reward: float32 [16], P(('grp', 'img', 'rows')), parts along dimension 0
There are 2 independent parts, one for each index of `grp`. A program takes and returns all parts, laid end to end along the dimension named above; an argument that names none is the same for every part. Nothing has to cross between parts.
Inputs may be any that keep to these rules, and one draw needn't show every extreme that they name: Each row is a permutation: image g * 4 + j is scored in slot owner_slot[g, j] of its image group.
All inputs are finite; a program needn't handle non-finite values.
Results may differ from a plain program's by a relative error of at most 0.028.
Values may be sent and summed in bfloat16 or wider, within the bound.
A program may use at most 128 MiB of HBM per device.

v0:
```python
import math

import jax
import jax.numpy as jnp
from jax import lax
from jax.sharding import PartitionSpec as P

C = 128
GROUPS = 32
PATCH = 14
HEAD_DIM = 80
W = 112


EPS_GROUP = 1e-06
EPS_LAYER = 1e-05


def padded_2(block, sides, width):
    for axis, dim in sides:
        count = lax.axis_size(axis)
        forward = [(i, i + 1) for i in range(count - 1)]
        backward = [(target, source) for source, target in forward]
        low = lax.ppermute(
            lax.slice_in_dim(block, block.shape[dim] - width, None, axis=dim), axis, forward
        )
        high = lax.ppermute(lax.slice_in_dim(block, 0, width, axis=dim), axis, backward)
        block = jnp.concatenate([low, block, high], axis=dim)
    return block


def round_half(values):
    return lax.optimization_barrier(values.astype(jnp.bfloat16)).astype(jnp.float32)


def layer_norm(values, scale_vec):
    average = jnp.mean(values, axis=-1, keepdims=True)
    centred = values - average
    spread = jnp.mean(centred * centred, axis=-1, keepdims=True)
    inverse = lax.rsqrt(spread + EPS_LAYER)
    normed = centred * inverse
    return (normed * scale_vec, normed, inverse)


def layer_norm_back(upstream, normed, inverse, scale_vec):
    scaled = upstream * scale_vec
    mean_one = jnp.mean(scaled, axis=-1, keepdims=True)
    mean_two = jnp.mean(scaled * normed, axis=-1, keepdims=True)
    return inverse * (scaled - mean_one - normed * mean_two)


def silu_parts(values):
    sigmoid = jax.nn.sigmoid(values)
    return (values * sigmoid, sigmoid * (1.0 + values * (1.0 - sigmoid)))


def soft_weights(q_heads, k_heads):
    factor = 1.0 / math.sqrt(HEAD_DIM)
    scores = jnp.einsum("thd,shd->hts", q_heads, k_heads) * factor
    row_max = jnp.max(scores, axis=-1, keepdims=True)
    exp_scores = jnp.exp(scores - row_max)
    return exp_scores / jnp.sum(exp_scores, axis=-1, keepdims=True)


def split_heads(rows_in):
    return rows_in.reshape(rows_in.shape[0], rows_in.shape[1] // HEAD_DIM, HEAD_DIM).astype(
        jnp.float32
    )


def attend(queries, key_rows, value_rows):
    prob_soft = soft_weights(split_heads(queries), split_heads(key_rows))
    attended = jnp.einsum("hts,shd->thd", round_half(prob_soft), split_heads(value_rows))
    return attended.reshape(queries.shape).astype(jnp.bfloat16)


def attend_back(queries, key_rows, value_rows, head_grad):
    factor = 1.0 / math.sqrt(HEAD_DIM)
    q_heads = split_heads(queries)
    k_heads = split_heads(key_rows)
    v_heads = split_heads(value_rows)
    g_heads = split_heads(head_grad)
    prob_soft = soft_weights(q_heads, k_heads)
    dprob = jnp.einsum("thd,shd->hts", g_heads, v_heads)
    dvalue = (
        jnp.einsum("hts,thd->shd", round_half(prob_soft), g_heads)
        .reshape(queries.shape)
        .astype(jnp.bfloat16)
    )
    dscores = prob_soft * (dprob - jnp.sum(dprob * prob_soft, axis=-1, keepdims=True)) * factor
    dscores = round_half(dscores)
    dquery = (
        jnp.einsum("hts,shd->thd", dscores, k_heads).reshape(queries.shape).astype(jnp.bfloat16)
    )
    dkey = jnp.einsum("hts,thd->shd", dscores, q_heads).reshape(queries.shape).astype(jnp.bfloat16)
    return (dquery, dkey, dvalue)


def rows_total_sum(values):
    return lax.psum(values, "rows")


def head_total(values):
    return lax.psum(values.astype(jnp.bfloat16), "tp").astype(jnp.float32)


def regroup(values):
    return lax.all_to_all(values, "rows", split_axis=0, concat_axis=0, tiled=True)


def body(
    features,
    gn_gain,
    conv_w,
    patch_w,
    pos_emb,
    ln1_gain,
    qkv_w,
    out_w,
    final_gain,
    head_w,
    owner_slot,
):
    slab_imgs, rows_here, _, flat_width = features.shape
    col_count = W
    chan_count = flat_width // col_count
    row_devices = lax.axis_size("rows")
    rows_total = rows_here * row_devices
    groups_here = GROUPS * chan_count // C
    group_width = chan_count // groups_here
    count_group = rows_total * col_count * group_width
    own_count = slab_imgs // row_devices
    half_patch = PATCH // 2
    patch_rows = rows_total // half_patch
    patch_cols = col_count // half_patch

    def channel_group_sums(flat):
        per_col = jnp.sum(flat, axis=1).reshape(slab_imgs, col_count, chan_count)
        per_chan = jnp.sum(per_col, axis=1)
        return jnp.sum(per_chan.reshape(slab_imgs, groups_here, group_width), axis=2)

    def spread_flat(per_group):
        return jnp.tile(jnp.repeat(per_group, group_width, axis=1), (1, col_count))[:, None, :]

    feat_float = features.reshape(slab_imgs, rows_here, flat_width).astype(jnp.float32)
    stat_sums = rows_total_sum(
        jnp.stack([channel_group_sums(feat_float), channel_group_sums(feat_float * feat_float)])
    )
    average = stat_sums[0] / count_group
    inverse = lax.rsqrt(stat_sums[1] / count_group - average * average + EPS_GROUP)
    gain_flat = jnp.tile(gn_gain, col_count)[None, None, :]
    normed = (feat_float - spread_flat(average)) * spread_flat(inverse)
    scaled = normed * gain_flat
    active, slope_silu = silu_parts(scaled)
    active = active.astype(jnp.bfloat16)
    kernel_rows = conv_w.reshape(27, chan_count)
    widened = jnp.pad(active, ((0, 0), (2, 2), (0, 0)))
    block_rows = widened.shape[1]
    padded = jnp.pad(widened, ((0, 0), (0, 0), (chan_count, chan_count)))
    terms = lax.dot_general(
        kernel_rows,
        padded.reshape(-1, chan_count),
        (((1,), (1,)), ((), ())),
        preferred_element_type=jnp.float32,
    )
    shifted_terms = terms.reshape(3, 3, 3, slab_imgs, block_rows, col_count + 2)
    out_rows = rows_here + 2
    total = jnp.zeros((3, slab_imgs, out_rows, col_count), jnp.float32)
    for shifted_offset_y in range(3):
        for shifted_offset_x in range(3):
            total = (
                total
                + shifted_terms[
                    :,
                    shifted_offset_y,
                    shifted_offset_x,
                    :,
                    shifted_offset_y : shifted_offset_y + out_rows,
                    shifted_offset_x : shifted_offset_x + col_count,
                ]
            )
    edges = jnp.concatenate([total[:, :, :1], total[:, :, -1:]], axis=2)
    edges_rim = padded_2(edges, (("rows", 2),), 1)
    middle = total[:, :, 1:-1]
    partial_rgb = (
        middle.at[:, :, 0:1].add(edges_rim[:, :, 0:1]).at[:, :, -1:].add(edges_rim[:, :, 3:4])
    )
    picture = head_total(partial_rgb).astype(jnp.bfloat16)
    slot_of = owner_slot[0]
    slot_ids = jnp.arange(slab_imgs, dtype=jnp.int32)
    selector = (slot_of[None, :] == slot_ids[:, None]).astype(jnp.bfloat16)
    by_image = picture.transpose(1, 0, 2, 3).reshape(slab_imgs, -1)
    ordered = jnp.dot(selector, by_image, preferred_element_type=jnp.float32).astype(jnp.bfloat16)
    outgoing = ordered.reshape(row_devices, own_count, 3, rows_here, col_count)
    arrived = regroup(outgoing)
    owned_images = arrived.transpose(1, 2, 0, 3, 4).reshape(own_count, 3, rows_total, col_count)
    gathered = (
        lax.all_gather(qkv_w, "rows", axis=0, tiled=True),
        lax.all_gather(out_w, "rows", axis=0, tiled=True),
        lax.all_gather(patch_w, "rows", axis=0, tiled=True),
    )
    qkv_half = gathered[0]
    out_half = gathered[1]
    patch_full = gathered[2]
    entry_index = jnp.arange(3 * PATCH * PATCH, dtype=jnp.int32)
    colour = entry_index % 3
    pixel_index = entry_index // 3
    target = (
        colour * half_patch * half_patch
        + pixel_index // PATCH // 2 * half_patch
        + pixel_index % PATCH // 2
    )
    fold_table = (
        target[:, None] == jnp.arange(3 * half_patch * half_patch, dtype=jnp.int32)[None, :]
    ).astype(jnp.float32)
    folded_weight = jnp.dot(
        patch_full.astype(jnp.float32), fold_table, precision=lax.Precision.HIGHEST
    )

    def forward_one(picture_one):
        patch_cells = picture_one.reshape(
            3, patch_rows, half_patch, patch_cols, half_patch
        ).transpose(1, 3, 0, 2, 4)
        patch_cells = patch_cells.reshape(
            patch_rows * patch_cols, 3 * half_patch * half_patch
        ).astype(jnp.float32)
        embedded = jnp.dot(
            patch_cells, folded_weight.T, precision=lax.Precision.HIGHEST
        ) + pos_emb.astype(jnp.float32)
        normed_in, hat_in, inv_in = layer_norm(embedded, ln1_gain)
        normed_round = normed_in.astype(jnp.bfloat16)
        queries = jnp.dot(
            normed_round, qkv_half[:, 0, :], preferred_element_type=jnp.float32
        ).astype(jnp.bfloat16)
        key_rows = jnp.dot(
            normed_round, qkv_half[:, 1, :], preferred_element_type=jnp.float32
        ).astype(jnp.bfloat16)
        value_rows = jnp.dot(
            normed_round, qkv_half[:, 2, :], preferred_element_type=jnp.float32
        ).astype(jnp.bfloat16)
        attended = attend(queries, key_rows, value_rows)
        mixed_out = head_total(jnp.dot(attended, out_half.T, preferred_element_type=jnp.float32))
        residual_out = embedded + mixed_out
        pooled = jnp.mean(residual_out, axis=0)
        pooled_out, hat_z, inv_z = layer_norm(pooled, final_gain)
        reward = jnp.sum(pooled_out * head_w)
        return (reward, (hat_in, inv_in, queries, key_rows, value_rows, hat_z, inv_z))

    rewards, stored = lax.map(forward_one, owned_images)

    def backward_one(saved_one):
        hat_in, inv_in, queries, key_rows, value_rows, hat_z, inv_z = saved_one
        upstream = layer_norm_back(head_w, hat_z, inv_z, final_gain)
        row_round = upstream.astype(jnp.bfloat16)[None, :]
        head_grad = jnp.dot(row_round, out_half, preferred_element_type=jnp.float32).astype(
            jnp.bfloat16
        )
        head_grad = jnp.broadcast_to(head_grad, queries.shape)
        dquery, dkey, dvalue = attend_back(queries, key_rows, value_rows, head_grad)
        partial_value = jnp.dot(dquery, qkv_half[:, 0, :].T, preferred_element_type=jnp.float32)
        partial_value = partial_value + jnp.dot(
            dkey, qkv_half[:, 1, :].T, preferred_element_type=jnp.float32
        )
        partial_value = partial_value + jnp.dot(
            dvalue, qkv_half[:, 2, :].T, preferred_element_type=jnp.float32
        )
        dnormed = head_total(partial_value)
        dembedded = upstream[None, :] + layer_norm_back(dnormed, hat_in, inv_in, ln1_gain)
        cell_grads = jnp.dot(round_half(dembedded), folded_weight, precision=lax.Precision.HIGHEST)
        cell_grads = cell_grads.reshape(
            patch_rows, patch_cols, 3, half_patch, half_patch
        ).transpose(2, 0, 3, 1, 4)
        return cell_grads.reshape(3, rows_total, col_count).astype(jnp.bfloat16)

    back_owned = lax.map(backward_one, stored)
    outgoing_back = back_owned.reshape(own_count, 3, row_devices, rows_here, col_count).transpose(
        2, 0, 1, 3, 4
    )
    returned = regroup(outgoing_back)
    by_slot = returned.reshape(slab_imgs, -1)
    dpicture = jnp.dot(selector.T, by_slot, preferred_element_type=jnp.float32).astype(jnp.bfloat16)
    dpicture = dpicture.reshape(slab_imgs, 3, rows_here, col_count).transpose(1, 0, 2, 3)
    grad_rimmed = padded_2(dpicture, (("rows", 2),), 1)
    grad_padded = jnp.pad(grad_rimmed, ((0, 0), (0, 0), (0, 0), (1, 1)))
    windows = []
    for offset_y in range(3):
        for offset_x in range(3):
            windows.append(
                grad_padded[
                    :,
                    :,
                    2 - offset_y : 2 - offset_y + rows_here,
                    2 - offset_x : 2 - offset_x + col_count,
                ]
            )
    stacked = jnp.stack(windows, axis=1).reshape(27, -1)
    dactive = lax.dot_general(
        stacked, kernel_rows, (((0,), (0,)), ((), ())), preferred_element_type=jnp.float32
    )
    dactive = dactive.reshape(slab_imgs, rows_here, flat_width)
    gated_grad = dactive * slope_silu * gain_flat
    back_sums = rows_total_sum(
        jnp.stack([channel_group_sums(gated_grad), channel_group_sums(gated_grad * normed)])
    )
    back_one = back_sums[0] / count_group
    back_two = back_sums[1] / count_group
    grad_features = spread_flat(inverse) * (
        gated_grad - spread_flat(back_one) - normed * spread_flat(back_two)
    )
    grad_out = grad_features.astype(jnp.bfloat16).reshape(slab_imgs, rows_here, 1, flat_width)
    return (grad_out, rewards)


def solution(mesh):
    placed = (
        P(("grp", "img"), "rows", "tp", None),
        P("tp"),
        P(None, None, None, "tp"),
        P("rows", None),
        P(),
        P(),
        P("rows", None, "tp"),
        P("rows", "tp"),
        P(),
        P(),
        P(("grp", "img"), None),
    )
    return jax.shard_map(
        body,
        mesh=mesh,
        in_specs=placed,
        out_specs=(P(("grp", "img"), "rows", "tp", None), P(("grp", "img", "rows"))),
        check_vma=False,
    )
```

profile of v0, /device:TPU:0, one launch (start us, length us, event | category | flops | bytes accessed | tf_op | source)
XLA Modules:
  0.0 287.5 jit_solution(1016339752901137906)
XLA Ops:
  7.2 0.7 all-gather.4.cloned.1.call-update
  8.0 0.7 all-gather.6.cloned.1.call-update
  8.7 0.4 convert_reduce_fusion
  9.5 0.4 fusion.22
  10.3 13.6 %psum.37 = f32[2,4,16]{2,1,0:T(4,128)S(1)} all-reduce(f32[2,4,16]{2,1,0:T(4,128)S(1)} %pad_maximum_fusion.2), channel_id=1, replica_groups=mesh['grp'=2,'rows'=4,'img'=2,'tp'=2] {'rows'}, use_global_device_ids=true, to_apply=%region_6.0 | all-reduce | flops 128 | bytes 1024 | tf_op jit(solution)/shard_map/psum | solution.py:100
  24.6 0.3 fusion.32
  25.0 0.4 pad.30
  25.4 0.8 reshape.366
  26.3 0.6 convolution_bitcast_fusion
  26.9 1.2 reshape.368
  28.1 0.2 fusion.67
  28.3 1.3 collective-permute-start
  29.6 1.3 collective-permute-start.1
  31.0 4.7 %collective-permute-done.1 = f32[3,4,1,112]{3,2,1,0:T(1,128)S(1)} collective-permute-done((f32[3,4,1,112]{3,2,1,0:T(1,128)S(1)}, f32[3,4,1,112]{3,2,1,0:T(1,128)S(1)}, u32[]{:S(2)}, u32[]{:S(2)}) %collective-permute-start.1) | collective-permute-done | bytes 5408 | tf_op jit(solution)/shard_map/ppermute | solution.py:27
  36.0 3.4 %psum.38 = bf16[4,2352]{1,0:T(4,128)(2,1)S(1)} all-reduce(bf16[4,2352]{1,0:T(4,128)(2,1)S(1)} %reshape.369), channel_id=1, replica_groups=mesh['grp'=2,'rows'=4,'img'=2,'tp'=2] {'tp'}, use_global_device_ids=true, to_apply=%region_7.8 | all-reduce | flops 9408 | bytes 37632 | tf_op jit(solution)/shard_map/psum | solution.py:104
  39.5 0.7 reshape.370
  40.2 3.3 %all-to-all-start = ((bf16[4,1,3,7,112]{4,3,2,1,0:T(8,128)(2,1)}), bf16[4,1,3,7,112]{4,3,2,1,0:T(8,128)(2,1)S(1)}, u32[]{:S(2)}, u32[]{:S(2)}) async-start(bf16[4,1,3,7,112]{4,3,2,1,0:T(8,128)(2,1)} %bitcast.9), calls=%async_computation | async-start | bytes 49152 | tf_op jit(solution)/shard_map/all_to_all | solution.py:108
  43.6 5.6 %all-to-all-done = bf16[4,1,3,7,112]{4,3,2,1,0:T(8,128)(2,1)S(1)} async-done(((bf16[4,1,3,7,112]{4,3,2,1,0:T(8,128)(2,1)}), bf16[4,1,3,7,112]{4,3,2,1,0:T(8,128)(2,1)S(1)}, u32[]{:S(2)}, u32[]{:S(2)}) %all-to-all-start) | async-done | bytes 18848 | tf_op jit(solution)/shard_map/all_to_all | solution.py:108
  49.2 0.4 reshape.371
  49.6 0.6 copy.48
  50.5 0.7 all-gather.4.cloned.1.call-done
  51.1 2.3 fusion.56
  53.4 0.5 fusion.126
  54.3 89.8 %all-gather.6.cloned.1.call-done = bf16[1280,3,640]{2,0,1:T(8,128)(2,1)} async-done(((bf16[320,3,640]{2,0,1:T(8,128)(2,1)}), bf16[1280,3,640]{2,0,1:T(8,128)(2,1)}) %all-gather.6.cloned.1.call-update) | async-done | bytes 4915216 | tf_op jit(solution)/shard_map/all_gather | solution.py:198
  144.2 1.8 fusion.20
  146.2 1.9 fusion.19
  148.3 0.2 fusion.127
  148.6 1.9 fusion.21
  150.7 0.2 fusion.15
  151.0 0.8 convert_element_type.190
  151.8 30.6 %all-gather.8.cloned.1.call-done = bf16[1280,640]{1,0:T(8,128)(2,1)} async-done(((bf16[320,640]{1,0:T(8,128)(2,1)}), bf16[1280,640]{1,0:T(8,128)(2,1)}) %all-gather.8.cloned.1.call-update) | async-done | bytes 1638416 | tf_op jit(solution)/shard_map/all_gather | solution.py:199
  182.4 2.9 convolution_convert_fusion.2
  185.3 0.2 all-reduce.8.cloned.1.call-start
  185.5 16.8 %all-reduce.6.cloned.1.call-done = bf16[64,1280]{1,0:T(8,128)(2,1)} async-done(((bf16[64,1280]{1,0:T(8,128)(2,1)}), bf16[64,1280]{1,0:T(8,128)(2,1)}) %all-reduce.6.cloned.1.call-update) | async-done | bytes 163856 | tf_op jit(solution)/shard_map/while/body/eval_jaxpr/psum | solution.py:104
  202.3 1.0 add_reduce_fusion
  203.3 0.6 multiply_reduce_fusion.6
  204.5 0.6 multiply_reduce_fusion.5
  205.8 1.9 multiply_reduce_fusion.3
  209.0 1.3 fusion.123
  210.3 0.3 convolution_reduce_fusion
  210.9 1.1 fusion.60
  212.0 1.2 fusion.12
  213.4 0.2 fusion.16
  214.4 2.0 fusion.4
  216.4 2.0 convolution_add_fusion.1
  218.5 2.7 fusion.2
  221.2 19.3 %all-reduce.8.cloned.1.call-done = bf16[64,1280]{1,0:T(8,128)(2,1)} async-done(((bf16[64,1280]{1,0:T(8,128)(2,1)}), bf16[64,1280]{1,0:T(8,128)(2,1)}) %all-reduce.8.cloned.1.call-update) | async-done | bytes 163856 | tf_op jit(solution)/shard_map/while/body/eval_jaxpr/psum | solution.py:104
  240.6 1.1 fusion.55
  241.7 1.1 add_convert_fusion
  242.8 0.6 convolution_convert_fusion.7
  243.7 0.6 copy.62
  244.3 0.3 convert_element_type.211
  244.7 10.3 %all_to_all.10 = bf16[4,1,3,7,112]{4,3,2,1,0:T(8,128)(2,1)S(1)} all-to-all(bf16[4,1,3,7,112]{4,3,2,1,0:T(8,128)(2,1)S(1)} %copy.63), channel_id=1, replica_groups=mesh['grp'=2,'rows'=4,'img'=2,'tp'=2] {'rows'}, dimensions={0} | all-to-all | bytes 37632 | tf_op jit(solution)/shard_map/all_to_all | solution.py:108
  255.4 2.6 collective-permute-start.2
  258.0 1.3 collective-permute-start.3
  259.3 4.2 %collective-permute-done.3 = bf16[3,4,1,112]{3,2,0,1:T(2,128)(2,1)S(1)} collective-permute-done((bf16[3,4,1,112]{3,2,0,1:T(2,128)(2,1)S(1)}, bf16[3,4,1,112]{3,2,0,1:T(2,128)(2,1)S(1)}, u32[]{:S(2)}, u32[]{:S(2)}) %collective-permute-start.3) | collective-permute-done | bytes 2720 | tf_op jit(solution)/shard_map/ppermute | solution.py:27
  264.1 0.3 reshape.378
  264.5 0.4 fusion.132
  264.9 1.4 reshape.380
  266.3 0.5 reshape.379
  266.7 2.2 fusion.122
  269.7 8.9 %psum.41 = f32[2,4,16]{2,1,0:T(4,128)S(1)} all-reduce(f32[2,4,16]{2,1,0:T(4,128)S(1)} %pad_maximum_fusion.3), channel_id=1, replica_groups=mesh['grp'=2,'rows'=4,'img'=2,'tp'=2] {'rows'}, use_global_device_ids=true, to_apply=%region_28.29 | all-reduce | flops 128 | bytes 1024 | tf_op jit(solution)/shard_map/psum | solution.py:100
  279.3 0.6 fusion.53
  279.9 1.1 copy.67
  (144 shorter events, 7.1 us)
Async XLA Ops:
  7.2 1.5 copy-start
  7.2 44.0 %all-gather.4.cloned.1.call-start = ((), (), s32[]{:S(2)}) async-start(), calls=%async_computation.2 | async-start | bytes 2048000 | tf_op jit(solution)/shard_map/all_gather | solution.py:200
  7.9 136.3 %all-gather.6.cloned.1.call-start = ((), (), s32[]{:S(2)}) async-start(), calls=%async_computation.3 | async-start | bytes 6144000 | tf_op jit(solution)/shard_map/all_gather | solution.py:198
  8.7 173.7 %all-gather.8.cloned.1.call-start = ((), (), s32[]{:S(2)}) async-start(), calls=%async_computation.4 | async-start | bytes 2048000 | tf_op jit(solution)/shard_map/all_gather | solution.py:199
  9.1 15.4 %copy-start.21 = (f32[64]{0:T(128)S(1)}, f32[64]{0:T(128)}, u32[]{:S(2)}) copy-start(f32[64]{0:T(128)} %param.16) | copy-start | bytes 772
  25.0 1.3 copy-start.13
  26.3 1.8 copy-start.10
  26.9 12.5 %copy-start.19 = (s32[1,4]{1,0:T(1,128)S(1)}, s32[1,4]{1,0:T(1,128)}, u32[]{:S(2)}) copy-start(s32[1,4]{1,0:T(1,128)} %param.25) | copy-start | bytes 52
  28.3 2.6 collective-permute-start
  29.6 6.1 %collective-permute-start.1 = (f32[3,4,1,112]{3,2,1,0:T(1,128)S(1)}, f32[3,4,1,112]{3,2,1,0:T(1,128)S(1)}, u32[]{:S(2)}, u32[]{:S(2)}) collective-permute-start(f32[3,4,1,112]{3,2,1,0:T(1,128)S(1)} %get-tuple-element.136), channel_id=1, source_target_pairs={{4,0},{8,4},{12,8},{5,1},{9,5},{13,9},{6,2},{10,6},{14,10},{7,3},{... | collective-permute-start | bytes 16136 | tf_op jit(solution)/shard_map/ppermute | solution.py:27
  40.2 9.0 %all-to-all-start = ((bf16[4,1,3,7,112]{4,3,2,1,0:T(8,128)(2,1)}), bf16[4,1,3,7,112]{4,3,2,1,0:T(8,128)(2,1)S(1)}, u32[]{:S(2)}, u32[]{:S(2)}) async-start(bf16[4,1,3,7,112]{4,3,2,1,0:T(8,128)(2,1)} %bitcast.9), calls=%async_computation | async-start | bytes 49152 | tf_op jit(solution)/shard_map/all_to_all | solution.py:108
  43.5 158.8 %all-reduce.6.cloned.1.call-start = ((), (), s32[]{:S(2)}) async-start(), calls=%async_computation.5 | async-start | bytes 327680 | tf_op jit(solution)/shard_map/while/body/eval_jaxpr/psum | solution.py:104
  49.6 3.8 %copy-start.8 = (bf16[64,1280]{1,0:T(8,128)(2,1)S(1)}, bf16[64,1280]{1,0:T(8,128)(2,1)}, u32[]{:S(2)}) copy-start(bf16[64,1280]{1,0:T(8,128)(2,1)} %param.19) | copy-start | bytes 491524
  50.5 3.8 %copy-start.9 = (f32[1280]{0:T(1024)S(1)}, f32[1280]{0:T(1024)}, u32[]{:S(2)}) copy-start(f32[1280]{0:T(1024)} %param.20) | copy-start | bytes 15364
  54.0 94.1 %copy-start.14 = (f32[64]{0:T(128)}, f32[64]{0:T(128)S(1)}, u32[]{:S(2)}) copy-start(f32[64]{0:T(128)S(1)} %broadcast_multiply_fusion.2) | copy-start | bytes 772
  54.2 93.9 %copy-start.16 = (f32[64]{0:T(128)}, f32[64]{0:T(128)S(1)}, u32[]{:S(2)}) copy-start(f32[64]{0:T(128)S(1)} %add_rsqrt_fusion) | copy-start | bytes 772
  146.2 2.4 copy-start.3
  148.3 2.2 copy-start.5
  148.5 2.1 copy-start.7
  148.5 2.5 copy-start.18
  150.7 1.1 copy-start.2
  182.4 27.9 %copy-start.1 = (bf16[1280,640]{1,0:T(8,128)(2,1)S(1)}, bf16[1280,640]{1,0:T(8,128)(2,1)}, u32[]{:S(2)}) copy-start(bf16[1280,640]{1,0:T(8,128)(2,1)} %all-gather.8.cloned.1.call-done) | copy-start | bytes 4915204
  185.3 55.3 %all-reduce.8.cloned.1.call-start = ((), (), s32[]{:S(2)}) async-start(), calls=%async_computation.6 | async-start | bytes 327680 | tf_op jit(solution)/shard_map/while/body/eval_jaxpr/psum | solution.py:104
  210.6 2.6 copy-start.4
  210.6 2.8 copy-start.6
  218.4 22.1 %copy-start.15 = (f32[64]{0:T(128)S(1)}, f32[64]{0:T(128)}, u32[]{:S(2)}) copy-start(f32[64]{0:T(128)} %copy-done.14) | copy-start | bytes 772
  218.4 22.1 %copy-start.17 = (f32[64]{0:T(128)S(1)}, f32[64]{0:T(128)}, u32[]{:S(2)}) copy-start(f32[64]{0:T(128)} %copy-done.16) | copy-start | bytes 772
  218.5 23.3 %copy-start.12 = (f32[1280]{0:T(1024)S(1)}, f32[1280]{0:T(1024)}, u32[]{:S(2)}) copy-start(f32[1280]{0:T(1024)} %get-tuple-element.134) | copy-start | bytes 15364
  221.2 33.8 %copy-start.20 = (s32[1,4]{1,0:T(1,128)S(1)}, s32[1,4]{1,0:T(1,128)}, u32[]{:S(2)}) copy-start(s32[1,4]{1,0:T(1,128)} %param.25) | copy-start | bytes 52
  242.8 21.6 %copy-start.11 = (bf16[27,64]{1,0:T(8,128)(2,1)S(1)}, bf16[27,64]{1,0:T(8,128)(2,1)}, u32[]{:S(2)}) copy-start(bf16[27,64]{1,0:T(8,128)(2,1)} %copy-done.10) | copy-start | bytes 10372
  255.4 3.9 %collective-permute-start.2 = (bf16[3,4,1,112]{3,2,0,1:T(2,128)(2,1)S(1)}, bf16[3,4,1,112]{3,2,0,1:T(2,128)(2,1)S(1)}, u32[]{:S(2)}, u32[]{:S(2)}) collective-permute-start(bf16[3,4,1,112]{3,2,0,1:T(2,128)(2,1)S(1)} %get-tuple-element.138), channel_id=1, source_target_pairs={{0,4},{4,8},{8,12},{1,5},{5,9},{9,13},{2,6},{6,10},{10,14},{3,7},{... | collective-permute-start | bytes 8072 | tf_op jit(solution)/shard_map/ppermute | solution.py:24
  258.0 5.5 %collective-permute-start.3 = (bf16[3,4,1,112]{3,2,0,1:T(2,128)(2,1)S(1)}, bf16[3,4,1,112]{3,2,0,1:T(2,128)(2,1)S(1)}, u32[]{:S(2)}, u32[]{:S(2)}) collective-permute-start(bf16[3,4,1,112]{3,2,0,1:T(2,128)(2,1)S(1)} %get-tuple-element.139), channel_id=1, source_target_pairs={{4,0},{8,4},{12,8},{5,1},{9,5},{13,9},{6,2},{10,6},{14,10},{7,3},{... | collective-permute-start | bytes 8072 | tf_op jit(solution)/shard_map/ppermute | solution.py:27
Sparse Core Ops, SparseCore 0:
  9.6 41.5 all-gather.3
  52.7 91.4 all-gather.5
  145.7 36.5 all-gather.7
  185.4 16.8 all-reduce.5
  221.3 19.1 all-reduce.7
where the time goes:
time: 288 us
  waiting for transfers between devices  173 us (60%)
  blocking collectives  36.1 us (13%)
  matrix products  22.4 us (8%)
  between operations  17.2 us (6%)
  local copies, waits for them, and re-layouts  14.3 us (5%)
  other arithmetic  14.2 us (5%)
  starting transfers between devices  10.1 us (4%)
    all_gather x1, waiting for transfers between devices, body(): lax.all_gather(qkv_w, 'rows', axis=0, tiled=True)  89.8 us
    psum x2, waiting for transfers between devices, head_total(): return lax.psum(values.astype(jnp.bfloat16), 'tp').astype(jnp.float32)  36.1 us
    all_gather x1, waiting for transfers between devices, body(): lax.all_gather(out_w, 'rows', axis=0, tiled=True)  30.6 us
    psum x2, blocking collectives, rows_total_sum(): return lax.psum(values, 'rows')  22.4 us
    all_to_all x1, blocking collectives, regroup(): lax.all_to_all(values, 'rows', split_axis=0, concat_axis=0, tiled=True)  10.3 us
    ppermute x2, waiting for transfers between devices, padded_2(): lax.ppermute(lax.slice_in_dim(block, 0, width, axis=dim), axis, backward)  8.91 us
  transfers between devices with their start and end apart: 10, of which 8 were waited for; matrix products, arithmetic and copies ran while one was open for 7% of the time, Pallas kernels for 0%

commit v1 on v0

v1 whole, which is shorter than its diff:
```python
import functools
import math

import jax
import jax.numpy as jnp
from jax import lax
from jax.experimental import pallas as pl
from jax.experimental.pallas import tpu as pltpu
from jax.sharding import PartitionSpec as P

C = 128
GROUPS = 32
PATCH = 14
HEAD_DIM = 80
W = 112


EPS_GROUP = 1e-06
EPS_LAYER = 1e-05


def exchange_kernel(axes, sizes, pick, x_ref, o_ref, send_sems, recv_sems, local_sem):
    total = math.prod(sizes)
    me = 0
    for axis, size in zip(axes, sizes):
        me = me * size + lax.axis_index(axis)

    def place(offset):
        index = lax.rem(me + offset, total)
        rest = index
        where = {}
        for axis, size in reversed(list(zip(axes, sizes))):
            where[axis] = lax.rem(rest, size)
            rest = rest // size
        return index, where

    def chunk(index):
        return x_ref if pick is None else x_ref.at[index // pick]

    barrier = pltpu.get_barrier_semaphore()
    for offset in range(1, total):
        pl.semaphore_signal(
            barrier, inc=1, device_id=place(offset)[1], device_id_type=pl.DeviceIdType.MESH
        )
    own = pltpu.make_async_copy(chunk(me), o_ref.at[me], local_sem)
    own.start()
    pl.semaphore_wait(barrier, total - 1)
    copies = []
    for offset in range(1, total):
        index, where = place(offset)
        copy = pltpu.make_async_remote_copy(
            src_ref=chunk(index),
            dst_ref=o_ref.at[me],
            send_sem=send_sems.at[offset - 1],
            recv_sem=recv_sems.at[offset - 1],
            device_id=where,
            device_id_type=pl.DeviceIdType.MESH,
        )
        copy.start()
        copies.append(copy)
    own.wait()
    for copy in copies:
        copy.wait()


def exchange(values, axes, pick, ident):
    sizes = tuple(lax.axis_size(axis) for axis in axes)
    total = math.prod(sizes)
    item = values.shape if pick is None else values.shape[1:]
    size_out = total * math.prod(item) * values.dtype.itemsize
    space = pltpu.VMEM if size_out <= 4 * 2**20 else pl.ANY
    return pl.pallas_call(
        functools.partial(exchange_kernel, axes, sizes, pick),
        out_shape=jax.ShapeDtypeStruct((total,) + item, values.dtype),
        in_specs=[pl.BlockSpec(memory_space=space)],
        out_specs=pl.BlockSpec(memory_space=space),
        scratch_shapes=[
            pltpu.SemaphoreType.DMA((total - 1,)),
            pltpu.SemaphoreType.DMA((total - 1,)),
            pltpu.SemaphoreType.DMA,
        ],
        compiler_params=pltpu.CompilerParams(collective_id=ident, has_side_effects=True),
    )(values)


def round_half(values):
    return lax.optimization_barrier(values.astype(jnp.bfloat16)).astype(jnp.float32)


def layer_norm(values, scale_vec):
    average = jnp.mean(values, axis=-1, keepdims=True)
    centred = values - average
    spread = jnp.mean(centred * centred, axis=-1, keepdims=True)
    inverse = lax.rsqrt(spread + EPS_LAYER)
    normed = centred * inverse
    return (normed * scale_vec, normed, inverse)


def layer_norm_back(upstream, normed, inverse, scale_vec):
    scaled = upstream * scale_vec
    mean_one = jnp.mean(scaled, axis=-1, keepdims=True)
    mean_two = jnp.mean(scaled * normed, axis=-1, keepdims=True)
    return inverse * (scaled - mean_one - normed * mean_two)


def silu_parts(values):
    sigmoid = jax.nn.sigmoid(values)
    return (values * sigmoid, sigmoid * (1.0 + values * (1.0 - sigmoid)))


def fill(values, sizes):
    return jnp.pad(values, [(0, size - have) for size, have in zip(sizes, values.shape)])


def up16(count):
    return (count + 15) // 16 * 16


def attention(queries, key_rows):
    factor = 1.0 / math.sqrt(HEAD_DIM)
    scores = jnp.einsum("bthd,bshd->bhts", queries, key_rows, preferred_element_type=jnp.float32)
    scores = scores * factor
    row_max = jnp.max(scores, axis=-1, keepdims=True)
    exp_scores = jnp.exp(scores - row_max)
    return exp_scores / jnp.sum(exp_scores, axis=-1, keepdims=True)


def body(
    features,
    gn_gain,
    conv_w,
    patch_w,
    pos_emb,
    ln1_gain,
    qkv_w,
    out_w,
    final_gain,
    head_w,
    owner_slot,
):
    slab_imgs, rows_here, _, flat_width = features.shape
    col_count = W
    chan_count = flat_width // col_count
    row_devices = lax.axis_size("rows")
    rows_total = rows_here * row_devices
    groups_here = GROUPS * chan_count // C
    group_width = chan_count // groups_here
    count_group = rows_total * col_count * group_width
    half_patch = PATCH // 2
    patch_rows = rows_total // half_patch
    patch_cols = col_count // half_patch

    tp_devices = lax.axis_size("tp")
    feat_own, _, half_width = qkv_w.shape
    width = pos_emb.shape[1]
    heads_half = half_width // HEAD_DIM
    split_axes = ("grp", "img")
    if heads_half % (lax.axis_size("grp") * lax.axis_size("img")):
        split_axes = ("img",)
    planes = math.prod(lax.axis_size(axis) for axis in split_axes)
    plane_index = 0
    for axis in split_axes:
        plane_index = plane_index * lax.axis_size(axis) + lax.axis_index(axis)
    heads_mine = heads_half // planes
    span = heads_mine * HEAD_DIM
    cell_entries = 3 * half_patch * half_patch
    entry_index = jnp.arange(3 * PATCH * PATCH, dtype=jnp.int32)
    pixel_index = entry_index // 3
    target = (
        entry_index % 3 * half_patch * half_patch
        + pixel_index // PATCH // 2 * half_patch
        + pixel_index % PATCH // 2
    )
    fold_table = (
        target[:, None] == jnp.arange(cell_entries, dtype=jnp.int32)[None, :]
    ).astype(jnp.bfloat16)
    folded_own = jnp.dot(patch_w, fold_table, preferred_element_type=jnp.float32)
    weights_own = jnp.concatenate(
        [
            lax.dynamic_slice_in_dim(qkv_w, plane_index * span, span, 2).reshape(feat_own, 3 * span),
            lax.dynamic_slice_in_dim(out_w, plane_index * span, span, 1),
            folded_own.astype(jnp.bfloat16),
        ],
        axis=1,
    )
    weights_wide = (4 * span + cell_entries + 127) // 128 * 128
    weights = lax.all_gather(
        fill(weights_own, (feat_own, weights_wide)), "rows", axis=0, tiled=True
    )
    qkv_cols = weights[:, : 3 * span]
    out_cols = weights[:, 3 * span : 4 * span]
    folded_weight = weights[:, 4 * span : 4 * span + cell_entries]

    def channel_group_sums(flat):
        per_col = jnp.sum(flat, axis=1).reshape(slab_imgs, col_count, chan_count)
        per_chan = jnp.sum(per_col, axis=1)
        return jnp.sum(per_chan.reshape(slab_imgs, groups_here, group_width), axis=2)

    def rows_total_sum(values, ident):
        flat = fill(values.reshape(2 * slab_imgs, groups_here), (2 * slab_imgs, 128))
        summed = jnp.sum(exchange(flat, ("rows",), None, ident), axis=0)
        return summed[:, :groups_here].reshape(2, slab_imgs, groups_here)

    def spread_flat(per_group):
        return jnp.tile(jnp.repeat(per_group, group_width, axis=1), (1, col_count))[:, None, :]

    feat_float = features.reshape(slab_imgs, rows_here, flat_width).astype(jnp.float32)
    stat_sums = rows_total_sum(
        jnp.stack([channel_group_sums(feat_float), channel_group_sums(feat_float * feat_float)]), 1
    )
    average = stat_sums[0] / count_group
    inverse = lax.rsqrt(stat_sums[1] / count_group - average * average + EPS_GROUP)
    gain_flat = jnp.tile(gn_gain, col_count)[None, None, :]
    normed = (feat_float - spread_flat(average)) * spread_flat(inverse)
    scaled = normed * gain_flat
    active, slope_silu = silu_parts(scaled)
    active = active.astype(jnp.bfloat16)
    kernel_rows = conv_w.reshape(27, chan_count)
    widened = jnp.pad(active, ((0, 0), (2, 2), (0, 0)))
    block_rows = widened.shape[1]
    padded = jnp.pad(widened, ((0, 0), (0, 0), (chan_count, chan_count)))
    terms = lax.dot_general(
        kernel_rows,
        padded.reshape(-1, chan_count),
        (((1,), (1,)), ((), ())),
        preferred_element_type=jnp.float32,
    )
    shifted_terms = terms.reshape(3, 3, 3, slab_imgs, block_rows, col_count + 2)
    out_rows = rows_here + 2
    total = jnp.zeros((3, slab_imgs, out_rows, col_count), jnp.float32)
    for shifted_offset_y in range(3):
        for shifted_offset_x in range(3):
            total = (
                total
                + shifted_terms[
                    :,
                    shifted_offset_y,
                    shifted_offset_x,
                    :,
                    shifted_offset_y : shifted_offset_y + out_rows,
                    shifted_offset_x : shifted_offset_x + col_count,
                ]
            )
    mine = lax.axis_index("rows")
    tokens = patch_rows * patch_cols
    rim_entries = 3 * out_rows
    slot_of = owner_slot[0]
    slot_ids = jnp.arange(slab_imgs, dtype=jnp.int32)
    selector = (slot_of[None, :] == slot_ids[:, None]).astype(jnp.bfloat16)
    partial = total.transpose(1, 0, 2, 3).reshape(slab_imgs, -1).astype(jnp.bfloat16)
    ordered = jnp.dot(selector, partial, preferred_element_type=jnp.float32).astype(jnp.bfloat16)
    ordered = ordered.reshape(slab_imgs, rim_entries, col_count)
    slabs = exchange(
        fill(ordered, (slab_imgs, up16(rim_entries), 128)),
        ("rows",) + split_axes + ("tp",),
        planes * tp_devices,
        2,
    )
    slabs = slabs[:, :rim_entries, :col_count].astype(jnp.float32)
    slabs = slabs.reshape(row_devices, planes, tp_devices, 3, out_rows, col_count)
    slabs = jnp.sum(slabs, axis=2)
    middle = slabs[:, :, :, 1:-1]
    above = jnp.pad(slabs[:-1, :, :, -1:], ((1, 0), (0, 0), (0, 0), (0, rows_here - 1), (0, 0)))
    below = jnp.pad(slabs[1:, :, :, :1], ((0, 1), (0, 0), (0, 0), (rows_here - 1, 0), (0, 0)))
    picture = (middle + above + below).astype(jnp.bfloat16)

    patch_cells = picture.reshape(
        patch_rows, planes, 3, half_patch, patch_cols, half_patch
    ).transpose(1, 0, 4, 2, 3, 5)
    patch_cells = patch_cells.reshape(planes * tokens, cell_entries)
    embedded = lax.dot_general(
        patch_cells, folded_weight, (((1,), (1,)), ((), ())), preferred_element_type=jnp.float32
    ).reshape(planes, tokens, width) + pos_emb.astype(jnp.float32)
    normed_in, hat_in, inv_in = layer_norm(embedded, ln1_gain)
    pooled_in = jnp.mean(embedded, axis=1)
    qkv = jnp.dot(
        normed_in.astype(jnp.bfloat16).reshape(planes * tokens, width),
        qkv_cols,
        preferred_element_type=jnp.float32,
    ).astype(jnp.bfloat16)
    qkv = qkv.reshape(planes, tokens, 3, heads_mine, HEAD_DIM)
    queries, key_rows, value_rows = qkv[:, :, 0], qkv[:, :, 1], qkv[:, :, 2]
    prob_soft = attention(queries, key_rows)
    prob_columns = jnp.sum(round_half(prob_soft), axis=2)
    value_float = value_rows.astype(jnp.float32)
    attended_mean = jnp.sum(
        (prob_columns / tokens).transpose(0, 2, 1)[..., None] * value_float, axis=1
    ).reshape(planes, span)
    attended_high = attended_mean.astype(jnp.bfloat16)
    attended_low = (attended_mean - attended_high.astype(jnp.float32)).astype(jnp.bfloat16)
    mixed = lax.dot_general(
        jnp.stack([attended_high, attended_low]).reshape(2 * planes, span),
        out_cols,
        (((1,), (1,)), ((), ())),
        preferred_element_type=jnp.float32,
    )
    mixed = jnp.sum(mixed.reshape(2, planes, width), axis=0)
    mixed = jnp.sum(exchange(mixed, split_axes + ("tp",), None, 3), axis=0)
    pooled_out, hat_z, inv_z = layer_norm(pooled_in + mixed, final_gain)
    rewards = jnp.sum(pooled_out * head_w, axis=-1)
    rewards = lax.dynamic_slice_in_dim(rewards, plane_index, 1)
    upstream = layer_norm_back(head_w, hat_z, inv_z, final_gain)
    head_grad = (
        jnp.dot(upstream.astype(jnp.bfloat16), out_cols, preferred_element_type=jnp.float32)
        .astype(jnp.bfloat16)
        .astype(jnp.float32)
        .reshape(planes, 1, heads_mine, HEAD_DIM)
    )
    dprob = jnp.sum(head_grad * value_float, axis=-1).transpose(0, 2, 1)[:, :, None, :]
    factor = 1.0 / math.sqrt(HEAD_DIM)
    dscores = prob_soft * (dprob - jnp.sum(dprob * prob_soft, axis=-1, keepdims=True)) * factor
    dscores = dscores.astype(jnp.bfloat16)
    dvalue = (prob_columns.transpose(0, 2, 1)[..., None] * head_grad).astype(jnp.bfloat16)
    dquery = jnp.einsum(
        "bhts,bshd->bthd", dscores, key_rows, preferred_element_type=jnp.float32
    ).astype(jnp.bfloat16)
    dkey = jnp.einsum(
        "bhts,bthd->bshd", dscores, queries, preferred_element_type=jnp.float32
    ).astype(jnp.bfloat16)
    dqkv = jnp.stack([dquery, dkey, dvalue], axis=2).reshape(planes * tokens, 3 * span)
    dnormed = lax.dot_general(
        dqkv, qkv_cols, (((1,), (1,)), ((), ())), preferred_element_type=jnp.float32
    ).reshape(planes, tokens, width)
    first = jnp.where(plane_index + lax.axis_index("tp") == 0, 1.0, 0.0)
    dembedded = (upstream * first)[:, None, :] + layer_norm_back(dnormed, hat_in, inv_in, ln1_gain)
    cell_grads = jnp.dot(
        dembedded.astype(jnp.bfloat16).reshape(planes * tokens, width),
        folded_weight,
        preferred_element_type=jnp.float32,
    ).astype(jnp.bfloat16)
    cell_grads = cell_grads.reshape(
        planes, patch_rows, patch_cols, 3, half_patch, half_patch
    ).transpose(0, 3, 1, 4, 2, 5)
    back_image = jnp.pad(
        cell_grads.reshape(planes, 3, rows_total, col_count), ((0, 0), (0, 0), (1, 1), (0, 0))
    )
    slabs_back = jnp.stack(
        [back_image[:, :, r * rows_here : r * rows_here + out_rows] for r in range(row_devices)]
    ).reshape(row_devices * planes, rim_entries, col_count)
    returned = exchange(
        fill(slabs_back, (row_devices * planes, up16(rim_entries), 128)),
        ("rows",) + split_axes + ("tp",),
        tp_devices,
        4,
    )
    returned = returned[:, :rim_entries, :col_count].astype(jnp.float32)
    by_slot = jnp.sum(
        returned.reshape(row_devices, planes * tp_devices, rim_entries * col_count), axis=1
    ).astype(jnp.bfloat16)
    dpicture = jnp.dot(selector.T, by_slot, preferred_element_type=jnp.float32).astype(jnp.bfloat16)
    grad_rimmed = dpicture.reshape(slab_imgs, 3, out_rows, col_count).transpose(1, 0, 2, 3)
    grad_padded = jnp.pad(grad_rimmed, ((0, 0), (0, 0), (0, 0), (1, 1)))
    windows = []
    for offset_y in range(3):
        for offset_x in range(3):
            windows.append(
                grad_padded[
                    :,
                    :,
                    2 - offset_y : 2 - offset_y + rows_here,
                    2 - offset_x : 2 - offset_x + col_count,
                ]
            )
    stacked = jnp.stack(windows, axis=1).reshape(27, -1)
    dactive = lax.dot_general(
        stacked, kernel_rows, (((0,), (0,)), ((), ())), preferred_element_type=jnp.float32
    )
    dactive = dactive.reshape(slab_imgs, rows_here, flat_width)
    gated_grad = dactive * slope_silu * gain_flat
    back_sums = rows_total_sum(
        jnp.stack([channel_group_sums(gated_grad), channel_group_sums(gated_grad * normed)]), 5
    )
    back_one = back_sums[0] / count_group
    back_two = back_sums[1] / count_group
    grad_features = spread_flat(inverse) * (
        gated_grad - spread_flat(back_one) - normed * spread_flat(back_two)
    )
    grad_out = grad_features.astype(jnp.bfloat16).reshape(slab_imgs, rows_here, 1, flat_width)
    return (grad_out, rewards)


def solution(mesh):
    placed = (
        P(("grp", "img"), "rows", "tp", None),
        P("tp"),
        P(None, None, None, "tp"),
        P("rows", None),
        P(),
        P(),
        P("rows", None, "tp"),
        P("rows", "tp"),
        P(),
        P(),
        P(("grp", "img"), None),
    )
    return jax.shard_map(
        body,
        mesh=mesh,
        in_specs=placed,
        out_specs=(P(("grp", "img"), "rows", "tp", None), P(("grp", "img", "rows"))),
        check_vma=False,
    )
```

time: 288 us -> 161 us (0.56)
  waiting for transfers between devices: 173 us -> 7.59 us
  Pallas kernels: 0 us -> 50.8 us
  blocking collectives: 36.1 us -> 0 us
  local copies, waits for them, and re-layouts: 14.3 us -> 46.9 us
  starting transfers between devices: 10.1 us -> 0.04 us
  other arithmetic: 14.2 us -> 19.6 us
  matrix products: 22.4 us -> 19.4 us
    all_gather x3 -> x1, waiting for transfers between devices: 121 us -> 7.58 us  [body(): lax.all_gather(fill(weights_own, (feat_own, weights_wide)), 'rows', axis=...]
    pallas_call x0 -> x5, Pallas kernels: none -> 50.8 us  [exchange(): pl.pallas_call(functools.partial(exchange_kernel, axes, sizes, pick), out...]
    psum x2 -> x0, waiting for transfers between devices: 36.1 us -> none  [head_total(): return lax.psum(values.astype(jnp.bfloat16), 'tp').astype(jnp.float32)]
    psum x3 -> x0, blocking collectives: 25.9 us -> none  [the longest x2 22.4 us: rows_total_sum(): return lax.psum(values, 'rows')]
    all_to_all x1 -> x0, blocking collectives: 10.3 us -> none  [regroup(): lax.all_to_all(values, 'rows', split_axis=0, concat_axis=0, tiled=True)]
    reshape x9 -> x11, local copies, waits for them, and re-layouts: 2.09 us -> 11.7 us  [the longest x2 4.36 us: body(): cell_grads.reshape(planes, patch_rows, patch_cols, 3, half_patch, half_pa...]
    ppermute x4 -> x0, waiting for transfers between devices: 8.94 us -> none  [the longest x2 8.91 us: padded_2(): lax.ppermute(lax.slice_in_dim(block, 0, width, axis=dim), axis, backward)]
    dot_general x17 -> x10, matrix products: 21 us -> 14.5 us  [the longest x1 2.21 us: body(): lax.dot_general(jnp.stack([attended_high, attended_low]).reshape(2 * plan...]
  transfers between devices with their start and end apart: 10 -> 1, of which waited for: 8 -> 1; matrix products, arithmetic and copies ran while one was open for 7% -> 15% of each run, Pallas kernels for 0% -> 16%
where the time goes in v1:
time: 161 us; the launch traced here: 160 us
  Pallas kernels  50.8 us (32%)
  local copies, waits for them, and re-layouts  46.9 us (29%)
  other arithmetic  19.6 us (12%)
  matrix products  19.4 us (12%)
  between operations  15.4 us (10%)
  waiting for transfers between devices  7.59 us (5%)
    pallas_call x5, Pallas kernels, exchange(): pl.pallas_call(functools.partial(exchange_kernel, axes, sizes, pick), out...  50.8 us
    all_gather x1, waiting for transfers between devices, body(): lax.all_gather(fill(weights_own, (feat_own, weights_wide)), 'rows', axis=...  7.58 us
    reshape x2, local copies, waits for them, and re-layouts, body(): cell_grads.reshape(planes, patch_rows, patch_cols, 3, half_patch, half_pa...  4.36 us
    unnamed x57, local copies, waits for them, and re-layouts  3.4 us
    pad x5, local copies, waits for them, and re-layouts, fill(): jnp.pad(values, [(0, size - have) for size, have in zip(sizes, values.sha...  3.38 us
  transfers between devices with their start and end apart: 1, of which 1 were waited for; matrix products, arithmetic and copies ran while one was open for 15% of the time, Pallas kernels for 16%

profile of v1, /device:TPU:0, one launch (start us, length us, event | category | flops | bytes accessed | tf_op | source)
XLA Modules:
  0.0 159.7 jit_solution(12901965436759272822)
XLA Ops:
  7.3 1.2 constant_dynamic-slice_fusion
  10.0 0.9 pad.49.clone
  12.6 0.6 pad.43.x_ref
  13.2 8.6 %shard_map.122 = f32[4,8,128]{2,1,0:T(8,128)} custom-call(f32[8,128]{1,0:T(8,128)} %pad.43.x_ref), custom_call_target="tpu_custom_call" | custom-call | tf_op jit(solution)/shard_map/pallas_call | solution.py:72
  21.8 0.7 reduce_sum.305
  23.9 1.4 pad.70
  25.2 2.0 %reshape.381 = bf16[5016,64]{1,0:T(8,128)(2,1)S(1)} reshape(bf16[4,11,7296]{2,1,0:T(8,128)(2,1)} %pad.70) | data formatting | bytes 1284096 | tf_op jit(solution)/shard_map/reshape | solution.py:224
  27.3 1.4 convolution_bitcast_fusion
  28.7 2.3 %reshape.383 = f32[3,3,3,4,11,114]{5,4,3,2,1,0:T(8,128)S(1)} reshape(f32[27,5016]{1,0:T(8,128)} %convolution_bitcast_fusion) | data formatting | bytes 1083456 | tf_op jit(solution)/shard_map/reshape | solution.py:228
  31.6 0.6 pad.46.x_ref
  32.2 16.5 %shard_map.123 = bf16[32,32,128]{2,1,0:T(8,128)(2,1)} custom-call(bf16[4,32,128]{2,1,0:T(8,128)(2,1)} %pad.46.x_ref), custom_call_target="tpu_custom_call" | custom-call | tf_op jit(solution)/shard_map/pallas_call | solution.py:72
  48.7 1.0 slice_convert_fusion
  50.0 0.7 reduce_sum.306
  50.7 0.7 copy.122
  51.4 2.5 %reshape.387 = bf16[4,4,3,7,16,7]{5,4,1,3,2,0:T(8,128)(2,1)S(1)} reshape(bf16[4,4,3,7,112]{4,1,3,2,0:T(4,128)(2,1)} %copy.122) | data formatting | bytes 150528 | tf_op jit(solution)/shard_map/reshape | solution.py:267
  54.0 3.1 %copy.123 = bf16[4,4,16,3,7,7]{2,1,5,4,3,0:T(4,128)(2,1)} copy(bf16[4,4,16,3,7,7]{5,2,0,4,3,1:T(8,128)(2,1)S(1)} %bitcast.172) | data formatting | bytes 150528 | tf_op jit(solution)/shard_map/transpose | solution.py:269
  57.1 2.1 %dot_general.51 = bf16[4,64,147]{1,2,0:T(8,128)(2,1)} reshape(bf16[4,4,16,3,7,7]{2,1,5,4,3,0:T(4,128)(2,1)} %copy.123) | data formatting | bytes 150528 | tf_op jit(solution)/shard_map/dot_general | solution.py:271
  59.2 0.6 fusion.118
  60.5 0.6 broadcast_subtract_fusion
  61.1 7.6 %all-gather.2.cloned.1.call-done = bf16[1280,896]{1,0:T(8,128)(2,1)} async-done(((bf16[320,896]{1,0:T(8,128)(2,1)}), bf16[1280,896]{1,0:T(8,128)(2,1)}) %all-gather.2.cloned.1.call-update) | async-done | bytes 2293776 | tf_op jit(solution)/shard_map/all_gather | solution.py:187
  68.6 1.8 %fusion.121 = (f32[4,64]{1,0:T(4,128)S(1)}, f32[4,64,1280]{2,1,0:T(8,128)S(1)}) fusion(f32[64,1280]{1,0:T(8,128)S(1)} %convert_element_type.169, bf16[4,64,147]{1,2,0:T(8,128)(2,1)} %dot_general.51, bf16[1280,896]{1,0:T(8,128)(2,1)} %all-gather.2.cloned.1.call-done), kind=kOutput, calls=%fused_computation.215 | convolution fusion | flops 96993024 | bytes 2450432 | tf_op jit(solution)/shard_map/dot_general | solution.py:271
  71.1 1.0 copy-done.2
  72.1 0.6 convolution_convert_fusion.2
  72.8 0.8 copy.130
  73.6 1.6 reshape.390
  75.2 0.9 fusion.119
  76.1 2.0 %fusion.122 = (bf16[4,2,64,64]{2,3,1,0:T(8,128)(2,1)}, f32[4,2,64,64]{2,3,1,0:T(8,128)}) fusion(bf16[4,64,1,2,80]{4,3,2,1,0:T(2,128)(2,1)} %get-tuple-element.26, bf16[4,64,1,2,80]{4,3,2,1,0:T(2,128)(2,1)} %get-tuple-element.25), kind=kOutput, calls=%fused_computation.216 | convolution fusion | flops 5375102 | bytes 360448 | tf_op jit(solution)/shard_map/div | solution.py:125
  78.0 1.0 convert_reduce_fusion.1
  79.1 0.6 copy.180
  79.7 0.8 copy.134
  80.5 1.2 fusion.64
  81.8 2.2 %convolution_reduce_fusion.x_ref = f32[4,1280]{1,0:T(4,128)} fusion(bf16[1280,896]{1,0:T(8,128)(2,1)} %all-gather.2.cloned.1.call-done, bf16[1,4,160]{2,1,0:T(4,128)(2,1)S(1)} %get-tuple-element.23, bf16[1,4,160]{2,1,0:T(4,128)(2,1)S(1)} %get-tuple-element.24), kind=kOutput, calls=%fused_computation.37 | convolution fusion | flops 3287040 | bytes 678400 | tf_op jit(solution)/shard_map/dot_general | solution.py:291
  84.0 7.0 %shard_map.124 = f32[8,4,1280]{2,1,0:T(4,128)} custom-call(f32[4,1280]{1,0:T(4,128)} %convolution_reduce_fusion.x_ref), custom_call_target="tpu_custom_call" | custom-call | tf_op jit(solution)/shard_map/pallas_call | solution.py:72
  91.0 1.0 reduce_sum.315
  92.3 1.4 multiply_reduce_fusion.3
  93.8 1.6 fusion.18
  95.4 1.0 fusion.65
  96.4 1.0 copy.136
  97.4 2.0 %fusion.16 = bf16[4,64,1,2,80]{4,1,3,0,2:T(8,128)(2,1)} fusion(f32[4,2,64,64]{2,3,1,0:T(8,128)} %get-tuple-element.40, f32[4,2,64]{2,1,0:T(2,128)S(1)} %copy.136, bf16[4,64,1,2,80]{4,3,2,1,0:T(2,128)(2,1)} %get-tuple-element.26), kind=kOutput, calls=%fused_computation.34 | convolution fusion | flops 5448255 | bytes 296960 | tf_op jit(solution)/shard_map/bhts,bthd->bshd/dot_general | solution.py:317
  99.5 2.1 %fusion.15 = bf16[4,64,1,2,80]{4,1,3,0,2:T(8,128)(2,1)} fusion(f32[4,2,64,64]{2,3,1,0:T(8,128)} %get-tuple-element.40, f32[4,2,64]{2,1,0:T(2,128)S(1)} %copy.136, bf16[4,64,1,2,80]{4,3,2,1,0:T(2,128)(2,1)} %get-tuple-element.25), kind=kOutput, calls=%fused_computation.33 | convolution fusion | flops 5448255 | bytes 296960 | tf_op jit(solution)/shard_map/bhts,bshd->bthd/dot_general | solution.py:314
  101.6 0.7 copy.138
  102.3 0.8 fusion.82
  103.2 1.1 pad_maximum_fusion.1
  104.3 1.2 copy.139
  105.4 1.3 dot_general.60
  106.8 2.0 %fusion.115 = (f32[4,64]{1,0:T(4,128)S(1)}, f32[4,64]{1,0:T(4,128)S(1)}, f32[4,64,1280]{2,1,0:T(8,128)S(1)}) fusion(f32[4,64]{1,0:T(4,128)S(1)} %copy-done.14, f32[4,64,1280]{2,1,0:T(8,128)S(1)} %get-tuple-element.38, f32[4,64]{1,0:T(4,128)S(1)} %copy-done.8, f32[1280]{0:T(1024)S(1)} %copy-done.10, bf16[4,64,480]{2,1,0:T(8,128)(2,1)S(1)} %dot_general.60, ...), kind=kOutput, calls=%fused_computation.209 | convolution fusion | flops 316538368 | bytes 4187136 | tf_op jit(solution)/shard_map/dot_general | solution.py:321
  109.3 1.5 convolution_convert_fusion.6
  110.8 1.2 reshape.393
  112.0 3.1 %copy.140 = bf16[4,4,16,3,7,7]{5,2,0,4,1,3:T(8,128)(2,1)S(1)} copy(bf16[4,4,16,3,7,7]{2,1,0,5,4,3:T(4,128)(2,1)} %reshape.393) | data formatting | bytes 150528 | tf_op jit(solution)/shard_map/reshape | solution.py:331
  115.1 1.4 reshape.394
  116.8 0.7 pad.51.x_ref
  117.5 10.1 %shard_map.125 = bf16[32,32,128]{2,1,0:T(8,128)(2,1)} custom-call(bf16[16,32,128]{2,1,0:T(8,128)(2,1)} %pad.51.x_ref), custom_call_target="tpu_custom_call" | custom-call | tf_op jit(solution)/shard_map/pallas_call | solution.py:72
  127.5 1.3 reshape.396
  130.0 1.0 reshape.399
  131.0 1.3 fusion.123
  132.3 1.4 reshape.400
  133.7 1.4 reshape.401
  135.2 2.3 %fusion.117 = (f32[4,7168]{1,0:T(4,128)S(1)}, f32[4,7168]{1,0:T(4,128)S(1)}) fusion(f32[4,7168]{1,0:T(4,128)S(1)} %tile.47, f32[4,7168]{1,0:T(4,128)} %copy-done.4, bf16[4,7,1,7168]{3,0,2,1:T(4,128)(2,1)S(1)} %copy-done.1, f32[4,7,7168]{2,1,0:T(8,128)} %reshape.401, f32[7168]{0:T(1024)S(1)} %mul.284), kind=kLoop, calls=%fused_computation.211 | loop fusion | flops 3153920 | bytes 1691648 | tf_op jit(solution)/shard_map/reduce_sum | solution.py:195
  138.3 0.6 pad.53.x_ref
  138.9 8.7 %shard_map.126 = f32[4,8,128]{2,1,0:T(8,128)} custom-call(f32[8,128]{1,0:T(8,128)} %pad.53.x_ref), custom_call_target="tpu_custom_call" | custom-call | tf_op jit(solution)/shard_map/pallas_call | solution.py:72
  147.6 0.7 reduce_sum.331
  148.9 0.8 tile.54
  149.7 1.5 fusion.50
  151.2 1.1 copy.146
  (138 shorter events, 10.4 us)
Async XLA Ops:
  7.2 1.4 copy-start
  7.2 1.9 %copy-start.22 = (bf16[320,588]{1,0:T(8,128)(2,1)S(1)}, bf16[320,588]{1,0:T(8,128)(2,1)}, u32[]{:S(2)}) copy-start(bf16[320,588]{1,0:T(8,128)(2,1)} %param.14) | copy-start | bytes 1128964
  7.2 61.5 %all-gather.2.cloned.1.call-start = ((), (), s32[]{:S(2)}) async-start(), calls=%async_computation | async-start | bytes 2867200 | tf_op jit(solution)/shard_map/all_gather | solution.py:187
  9.7 1.2 copy-start.1
  10.0 1.7 %copy-start.15 = (bf16[3,3,3,64]{3,2,1,0:T(4,128)(2,1)S(1)}, bf16[3,3,3,64]{3,2,1,0:T(4,128)(2,1)}, u32[]{:S(2)}) copy-start(bf16[3,3,3,64]{3,2,1,0:T(4,128)(2,1)} %param.13) | copy-start | bytes 10372
  10.0 1.7 %copy-start.20 = (f32[64]{0:T(128)S(1)}, f32[64]{0:T(128)}, u32[]{:S(2)}) copy-start(f32[64]{0:T(128)} %param.12) | copy-start | bytes 772
  11.9 11.4 %copy-start.6 = (bf16[64,1280]{1,0:T(8,128)(2,1)S(1)}, bf16[64,1280]{1,0:T(8,128)(2,1)}, u32[]{:S(2)}) copy-start(bf16[64,1280]{1,0:T(8,128)(2,1)} %param.15) | copy-start | bytes 491524
  23.2 0.6 copy-start.4
  28.7 2.7 %copy-start.16 = (s32[1,4]{1,0:T(1,128)S(1)}, s32[1,4]{1,0:T(1,128)}, u32[]{:S(2)}) copy-start(s32[1,4]{1,0:T(1,128)} %param.21) | copy-start | bytes 52
  53.9 5.3 %copy-start.11 = (f32[1280]{0:T(1024)S(1)}, f32[1280]{0:T(1024)}, u32[]{:S(2)}) copy-start(f32[1280]{0:T(1024)} %param.20) | copy-start | bytes 15364
  53.9 5.3 %copy-start.12 = (f32[1280]{0:T(1024)S(1)}, f32[1280]{0:T(1024)}, u32[]{:S(2)}) copy-start(f32[1280]{0:T(1024)} %param.19) | copy-start | bytes 15364
  61.1 9.8 %copy-start.9 = (f32[1280]{0:T(1024)S(1)}, f32[1280]{0:T(1024)}, u32[]{:S(2)}) copy-start(f32[1280]{0:T(1024)} %param.16) | copy-start | bytes 15364
  70.4 0.7 copy-start.7
  70.4 1.7 %copy-start.2 = (bf16[1280,896]{1,0:T(8,128)(2,1)S(1)}, bf16[1280,896]{1,0:T(8,128)(2,1)}, u32[]{:S(2)}) copy-start(bf16[1280,896]{1,0:T(8,128)(2,1)} %all-gather.2.cloned.1.call-done) | copy-start | bytes 6881284
  70.8 1.9 %copy-start.13 = (f32[4,64]{1,0:T(4,128)}, f32[4,64]{1,0:T(4,128)S(1)}, u32[]{:S(2)}) copy-start(f32[4,64]{1,0:T(4,128)S(1)} %add_rsqrt_fusion) | copy-start | bytes 3076
  92.3 1.4 copy-start.18
  95.3 7.0 %copy-start.19 = (f32[4]{0:T(128)S(1)}, f32[4]{0:T(128)}, u32[]{:S(2)}) copy-start(f32[4]{0:T(128)} %copy-done.18) | copy-start | bytes 52
  101.6 5.2 %copy-start.8 = (f32[4,64]{1,0:T(4,128)S(1)}, f32[4,64]{1,0:T(4,128)}, u32[]{:S(2)}) copy-start(f32[4,64]{1,0:T(4,128)} %copy-done.7) | copy-start | bytes 3076
  101.6 5.2 %copy-start.10 = (f32[1280]{0:T(1024)S(1)}, f32[1280]{0:T(1024)}, u32[]{:S(2)}) copy-start(f32[1280]{0:T(1024)} %param.16) | copy-start | bytes 15364
  101.6 5.2 %copy-start.14 = (f32[4,64]{1,0:T(4,128)S(1)}, f32[4,64]{1,0:T(4,128)}, u32[]{:S(2)}) copy-start(f32[4,64]{1,0:T(4,128)} %copy-done.13) | copy-start | bytes 3076
  116.5 12.5 %copy-start.17 = (s32[1,4]{1,0:T(1,128)S(1)}, s32[1,4]{1,0:T(1,128)}, u32[]{:S(2)}) copy-start(s32[1,4]{1,0:T(1,128)} %param.21) | copy-start | bytes 52
  137.5 12.2 %copy-start.3 = (f32[4,7,1,7168]{3,1,0,2:T(8,128)S(1)}, f32[4,7,1,7168]{3,1,0,2:T(8,128)}, u32[]{:S(2)}) copy-start(f32[4,7,1,7168]{3,1,0,2:T(8,128)} %reshape.400) | copy-start | bytes 2408452
  137.5 12.2 %copy-start.5 = (f32[4,7168]{1,0:T(4,128)S(1)}, f32[4,7168]{1,0:T(4,128)}, u32[]{:S(2)}) copy-start(f32[4,7168]{1,0:T(4,128)} %copy-done.4) | copy-start | bytes 344068
  149.7 2.6 %copy-start.21 = (f32[4]{0:T(128)S(1)}, f32[4]{0:T(128)}, u32[]{:S(2)}) copy-start(f32[4]{0:T(128)} %get-tuple-element.18) | copy-start | bytes 52
Sparse Core Ops, SparseCore 0:
  11.0 57.5 all-gather.1

commit v2 on v1

--- a/solution.py
+++ b/solution.py
@@ -116,13 +116,181 @@
     return (count + 15) // 16 * 16
 
 
-def attention(queries, key_rows):
+def mm(left, right, left_dim, right_dim):
+    return lax.dot_general(
+        left, right, (((left_dim,), (right_dim,)), ((), ())), preferred_element_type=jnp.float32
+    )
+
+
+def hold(values):
+    return values.astype(jnp.bfloat16)
+
+
+class Windows:
+    def __init__(self, span, heads_mine, cell_entries):
+        self.fold = (cell_entries + 127) // 128 * 128
+        self.heads = heads_mine
+        end = self.fold + 3 * span
+        self.wide = (end + span + 127) // 128 * 128
+        self.high = (end + 127) // 128 * 128
+        self.low = end // 128 * 128
+        self.end = end
+
+    def select(self, start, stop, first, blocks):
+        row = jnp.arange(start, stop, dtype=jnp.int32)[:, None]
+        column = jnp.arange(blocks * 128, dtype=jnp.int32)[None, :]
+        lane = column % 128
+        hit = (row == first + column // 128 * HEAD_DIM + lane) & (lane < HEAD_DIM)
+        return hit.astype(jnp.bfloat16)
+
+
+def over(count, step):
+    if count == 1:
+        step(0)
+    else:
+
+        @pl.loop(0, count)
+        def _(index):
+            step(index)
+
+
+def scorer_forward(
+    win, planes, tokens, per_chunk, cells_ref, w_ref, pick_qkv_ref, pick_out_ref, pos_ref, gain_ref,
+    hat_ref, inv_ref, heads_ref, prob_ref, mixed_ref, pooled_ref, att_ref,
+):
+    heads = win.heads
+    rows = per_chunk * tokens
     factor = 1.0 / math.sqrt(HEAD_DIM)
-    scores = jnp.einsum("bthd,bshd->bhts", queries, key_rows, preferred_element_type=jnp.float32)
-    scores = scores * factor
-    row_max = jnp.max(scores, axis=-1, keepdims=True)
-    exp_scores = jnp.exp(scores - row_max)
-    return exp_scores / jnp.sum(exp_scores, axis=-1, keepdims=True)
+
+    def embed(index):
+        at = pl.ds(pl.multiple_of(index * rows, rows), rows)
+        embedded = mm(cells_ref[at, :], w_ref[:, : win.fold], 1, 1)
+        width = embedded.shape[1]
+        embedded = embedded.reshape(per_chunk, tokens, width) + pos_ref[...].astype(jnp.float32)[None]
+        for inner in range(per_chunk):
+            pooled_ref[pl.ds(index * per_chunk + inner, 1), :] = jnp.mean(
+                embedded[inner], axis=0, keepdims=True
+            )
+        embedded = embedded.reshape(rows, width)
+        normed_in, hat, inverse = layer_norm(embedded, gain_ref[...])
+        hat_ref[at, :] = hat
+        inv_ref[at, :] = jnp.broadcast_to(inverse, (rows, 128))
+        flat = hold(mm(hold(normed_in), w_ref[:, win.fold : win.high], 1, 0))
+        heads_ref[at, :] = hold(mm(flat, pick_qkv_ref[...], 1, 0))
+
+    over(planes // per_chunk, embed)
+
+    def attend(plane):
+        at = pl.ds(pl.multiple_of(plane * tokens, tokens), tokens)
+        for head in range(heads):
+            query = heads_ref[at, head * 128 : head * 128 + 128]
+            key = heads_ref[at, (heads + head) * 128 : (heads + head) * 128 + 128]
+            value = heads_ref[at, (2 * heads + head) * 128 : (2 * heads + head) * 128 + 128]
+            scores = mm(query, key, 1, 1) * factor
+            exp_scores = jnp.exp(scores - jnp.max(scores, axis=-1, keepdims=True))
+            prob = exp_scores / jnp.sum(exp_scores, axis=-1, keepdims=True)
+            prob_ref[at, head * tokens : head * tokens + tokens] = prob
+            mean_row = (
+                jnp.sum(hold(prob).astype(jnp.float32), axis=0, keepdims=True) * (1.0 / tokens)
+            )
+            mean_high = hold(mean_row)
+            mean_low = hold(mean_row - mean_high.astype(jnp.float32))
+            att_ref[pl.ds(plane, 1), head * 128 : head * 128 + 128] = mm(
+                mean_high, value, 1, 0
+            ) + mm(mean_low, value, 1, 0)
+
+    if planes * heads <= 8 and tokens <= 64:
+        for plane in range(planes):
+            attend(plane)
+    else:
+        over(planes, attend)
+    attended = att_ref[...]
+    high = hold(attended)
+    low = hold(attended - high.astype(jnp.float32))
+    out_window = w_ref[:, win.low :]
+    mixed_ref[...] = mm(hold(mm(high, pick_out_ref[...], 1, 1)), out_window, 1, 1) + mm(
+        hold(mm(low, pick_out_ref[...], 1, 1)), out_window, 1, 1
+    )
+
+
+def scorer_backward(
+    win, planes, tokens, per_chunk, mixed_ref, pooled_ref, final_ref, head_w_ref, first_ref, w_ref,
+    pick_qkv_ref, pick_out_ref, gain_ref, hat_ref, inv_ref, heads_ref, prob_ref,
+    dcells_ref, reward_ref, grad_ref, up_ref, share_ref,
+):
+    heads = win.heads
+    rows = per_chunk * tokens
+    factor = 1.0 / math.sqrt(HEAD_DIM)
+    pooled = pooled_ref[...]
+    for index in range(mixed_ref.shape[0]):
+        pooled = pooled + mixed_ref[index]
+    final_gain = final_ref[...]
+    head_w = head_w_ref[...]
+    pooled_out, hat_z, inv_z = layer_norm(pooled, final_gain)
+    reward_ref[...] = jnp.broadcast_to(
+        jnp.sum(pooled_out * head_w, axis=-1, keepdims=True), reward_ref.shape
+    )
+    upstream = layer_norm_back(head_w, hat_z, inv_z, final_gain)
+    up_ref[...] = upstream * first_ref[0:1, 0:1]
+    share_ref[...] = mm(
+        hold(mm(hold(upstream), w_ref[:, win.low :], 1, 0)), pick_out_ref[...], 1, 0
+    )
+
+    def attend(plane):
+        at = pl.ds(pl.multiple_of(plane * tokens, tokens), tokens)
+        for head in range(heads):
+            lanes = [
+                slice((which * heads + head) * 128, (which * heads + head) * 128 + 128)
+                for which in range(3)
+            ]
+            query, key, value = (heads_ref[at, lane] for lane in lanes)
+            prob = prob_ref[at, head * tokens : head * tokens + tokens]
+            share = hold(
+                jnp.broadcast_to(
+                    share_ref[pl.ds(plane, 1), head * 128 : head * 128 + 128], (tokens, 128)
+                )
+            )
+            dprob = mm(share, value, 1, 1)
+            dscores = hold(
+                prob * (dprob - jnp.sum(dprob * prob, axis=-1, keepdims=True)) * factor
+            )
+            grad_ref[at, lanes[0]] = hold(mm(dscores, key, 1, 0))
+            grad_ref[at, lanes[1]] = hold(mm(dscores, query, 0, 0))
+            grad_ref[at, lanes[2]] = hold(mm(hold(prob), share, 0, 0))
+
+    if planes * heads <= 8 and tokens <= 64:
+        for plane in range(planes):
+            attend(plane)
+    else:
+        over(planes, attend)
+
+    def finish(index):
+        at = pl.ds(pl.multiple_of(index * rows, rows), rows)
+        flat = hold(mm(grad_ref[at, :], pick_qkv_ref[...], 1, 1))
+        dnormed = mm(flat, w_ref[:, win.fold : win.high], 1, 1)
+        dlinear = layer_norm_back(dnormed, hat_ref[at, :], inv_ref[at, 0:1], gain_ref[...])
+        width = dlinear.shape[1]
+        dlinear = dlinear.reshape(per_chunk, tokens, width)
+        pieces = [
+            dlinear[inner] + up_ref[pl.ds(index * per_chunk + inner, 1), :]
+            for inner in range(per_chunk)
+        ]
+        dembedded = hold(jnp.concatenate(pieces, axis=0) if per_chunk > 1 else pieces[0])
+        dcells_ref[at, :] = hold(mm(dembedded, w_ref[:, : win.fold], 1, 0))
+
+    over(planes // per_chunk, finish)
+
+
+def local_call(kernel, shapes, scratch, *operands):
+    vmem = pl.BlockSpec(memory_space=pltpu.VMEM)
+    return pl.pallas_call(
+        kernel,
+        out_shape=shapes,
+        in_specs=[vmem] * len(operands),
+        out_specs=[vmem] * len(shapes),
+        scratch_shapes=scratch,
+        compiler_params=pltpu.CompilerParams(vmem_limit_bytes=56 * 2**20),
+    )(*operands)
 
 
 def body(
@@ -175,21 +343,18 @@
         target[:, None] == jnp.arange(cell_entries, dtype=jnp.int32)[None, :]
     ).astype(jnp.bfloat16)
     folded_own = jnp.dot(patch_w, fold_table, preferred_element_type=jnp.float32)
+    win = Windows(span, heads_mine, cell_entries)
     weights_own = jnp.concatenate(
         [
+            fill(folded_own.astype(jnp.bfloat16), (feat_own, win.fold)),
             lax.dynamic_slice_in_dim(qkv_w, plane_index * span, span, 2).reshape(feat_own, 3 * span),
             lax.dynamic_slice_in_dim(out_w, plane_index * span, span, 1),
-            folded_own.astype(jnp.bfloat16),
         ],
         axis=1,
     )
-    weights_wide = (4 * span + cell_entries + 127) // 128 * 128
-    weights = lax.all_gather(
-        fill(weights_own, (feat_own, weights_wide)), "rows", axis=0, tiled=True
-    )
-    qkv_cols = weights[:, : 3 * span]
-    out_cols = weights[:, 3 * span : 4 * span]
-    folded_weight = weights[:, 4 * span : 4 * span + cell_entries]
+    weights = lax.all_gather(fill(weights_own, (feat_own, win.wide)), "rows", axis=0, tiled=True)
+    pick_qkv = win.select(win.fold, win.high, win.fold, 3 * heads_mine)
+    pick_out = win.select(win.low, win.wide, win.end, heads_mine)
 
     def channel_group_sums(flat):
         per_col = jnp.sum(flat, axis=1).reshape(slab_imgs, col_count, chan_count)
@@ -268,66 +433,57 @@
         patch_rows, planes, 3, half_patch, patch_cols, half_patch
     ).transpose(1, 0, 4, 2, 3, 5)
     patch_cells = patch_cells.reshape(planes * tokens, cell_entries)
-    embedded = lax.dot_general(
-        patch_cells, folded_weight, (((1,), (1,)), ((), ())), preferred_element_type=jnp.float32
-    ).reshape(planes, tokens, width) + pos_emb.astype(jnp.float32)
-    normed_in, hat_in, inv_in = layer_norm(embedded, ln1_gain)
-    pooled_in = jnp.mean(embedded, axis=1)
-    qkv = jnp.dot(
-        normed_in.astype(jnp.bfloat16).reshape(planes * tokens, width),
-        qkv_cols,
-        preferred_element_type=jnp.float32,
-    ).astype(jnp.bfloat16)
-    qkv = qkv.reshape(planes, tokens, 3, heads_mine, HEAD_DIM)
-    queries, key_rows, value_rows = qkv[:, :, 0], qkv[:, :, 1], qkv[:, :, 2]
-    prob_soft = attention(queries, key_rows)
-    prob_columns = jnp.sum(round_half(prob_soft), axis=2)
-    value_float = value_rows.astype(jnp.float32)
-    attended_mean = jnp.sum(
-        (prob_columns / tokens).transpose(0, 2, 1)[..., None] * value_float, axis=1
-    ).reshape(planes, span)
-    attended_high = attended_mean.astype(jnp.bfloat16)
-    attended_low = (attended_mean - attended_high.astype(jnp.float32)).astype(jnp.bfloat16)
-    mixed = lax.dot_general(
-        jnp.stack([attended_high, attended_low]).reshape(2 * planes, span),
-        out_cols,
-        (((1,), (1,)), ((), ())),
-        preferred_element_type=jnp.float32,
-    )
-    mixed = jnp.sum(mixed.reshape(2, planes, width), axis=0)
-    mixed = jnp.sum(exchange(mixed, split_axes + ("tp",), None, 3), axis=0)
-    pooled_out, hat_z, inv_z = layer_norm(pooled_in + mixed, final_gain)
-    rewards = jnp.sum(pooled_out * head_w, axis=-1)
-    rewards = lax.dynamic_slice_in_dim(rewards, plane_index, 1)
-    upstream = layer_norm_back(head_w, hat_z, inv_z, final_gain)
-    head_grad = (
-        jnp.dot(upstream.astype(jnp.bfloat16), out_cols, preferred_element_type=jnp.float32)
-        .astype(jnp.bfloat16)
-        .astype(jnp.float32)
-        .reshape(planes, 1, heads_mine, HEAD_DIM)
-    )
-    dprob = jnp.sum(head_grad * value_float, axis=-1).transpose(0, 2, 1)[:, :, None, :]
-    factor = 1.0 / math.sqrt(HEAD_DIM)
-    dscores = prob_soft * (dprob - jnp.sum(dprob * prob_soft, axis=-1, keepdims=True)) * factor
-    dscores = dscores.astype(jnp.bfloat16)
-    dvalue = (prob_columns.transpose(0, 2, 1)[..., None] * head_grad).astype(jnp.bfloat16)
-    dquery = jnp.einsum(
-        "bhts,bshd->bthd", dscores, key_rows, preferred_element_type=jnp.float32
-    ).astype(jnp.bfloat16)
-    dkey = jnp.einsum(
-        "bhts,bthd->bshd", dscores, queries, preferred_element_type=jnp.float32
-    ).astype(jnp.bfloat16)
-    dqkv = jnp.stack([dquery, dkey, dvalue], axis=2).reshape(planes * tokens, 3 * span)
-    dnormed = lax.dot_general(
-        dqkv, qkv_cols, (((1,), (1,)), ((), ())), preferred_element_type=jnp.float32
-    ).reshape(planes, tokens, width)
+    total_rows = planes * tokens
+    per_chunk = max(1, min(planes, 256 // tokens))
+    shape = jax.ShapeDtypeStruct
+    gain_row = ln1_gain[None]
+    hat_in, inv_in, head_cols, prob_soft, mixed, pooled_in = local_call(
+        functools.partial(scorer_forward, win, planes, tokens, per_chunk),
+        [
+            shape((total_rows, width), jnp.float32),
+            shape((total_rows, 128), jnp.float32),
+            shape((total_rows, 3 * heads_mine * 128), jnp.bfloat16),
+            shape((total_rows, heads_mine * tokens), jnp.float32),
+            shape((planes, width), jnp.float32),
+            shape((planes, width), jnp.float32),
+        ],
+        [pltpu.VMEM((planes, heads_mine * 128), jnp.float32)],
+        fill(patch_cells, (total_rows, win.fold)),
+        weights,
+        pick_qkv,
+        pick_out,
+        pos_emb,
+        gain_row,
+    )
+    mixed = exchange(mixed, split_axes + ("tp",), None, 3)
     first = jnp.where(plane_index + lax.axis_index("tp") == 0, 1.0, 0.0)
-    dembedded = (upstream * first)[:, None, :] + layer_norm_back(dnormed, hat_in, inv_in, ln1_gain)
-    cell_grads = jnp.dot(
-        dembedded.astype(jnp.bfloat16).reshape(planes * tokens, width),
-        folded_weight,
-        preferred_element_type=jnp.float32,
-    ).astype(jnp.bfloat16)
+    cell_grads, rewards = local_call(
+        functools.partial(scorer_backward, win, planes, tokens, per_chunk),
+        [
+            shape((total_rows, win.fold), jnp.bfloat16),
+            shape((planes, 128), jnp.float32),
+        ],
+        [
+            pltpu.VMEM((total_rows, 3 * heads_mine * 128), jnp.bfloat16),
+            pltpu.VMEM((planes, width), jnp.float32),
+            pltpu.VMEM((planes, heads_mine * 128), jnp.float32),
+        ],
+        mixed,
+        pooled_in,
+        final_gain[None],
+        head_w[None],
+        jnp.broadcast_to(first, (1, 128)),
+        weights,
+        pick_qkv,
+        pick_out,
+        gain_row,
+        hat_in,
+        inv_in,
+        head_cols,
+        prob_soft,
+    )
+    rewards = lax.dynamic_slice_in_dim(rewards[:, 0], plane_index, 1)
+    cell_grads = cell_grads[:, :cell_entries]
     cell_grads = cell_grads.reshape(
         planes, patch_rows, patch_cols, 3, half_patch, half_patch
     ).transpose(0, 3, 1, 4, 2, 5)

time: 161 us -> 140 us (0.87)
  matrix products: 19.4 us -> 4.68 us
  Pallas kernels: 50.8 us -> 64.5 us
  local copies, waits for them, and re-layouts: 46.9 us -> 37.5 us
  other arithmetic: 19.6 us -> 11.1 us
    dot_general x8 -> x0, matrix products: 13.9 us -> none  [the longest x1 2.21 us: body(): lax.dot_general(jnp.stack([attended_high, attended_low]).reshape(2 * plan...]
    pallas_call x0 -> x2, Pallas kernels: none -> 13.6 us  [local_call(): pl.pallas_call(kernel, out_shape=shapes, in_specs=[vmem] * len(operands),...]
    reduce_sum x9 -> x0, other arithmetic: 6.96 us -> none  [the longest x1 1.42 us: body(): rewards = jnp.sum(pooled_out * head_w, axis=-1)]
    dot_general x2 -> x0, local copies, waits for them, and re-layouts: 3.43 us -> none  [the longest x1 2.12 us: body(): lax.dot_general(patch_cells, folded_weight, (((1,), (1,)), ((), ())), pre...]
    reshape x2 -> x1, local copies, waits for them, and re-layouts: 4.36 us -> 1.23 us  [body(): cell_grads.reshape(planes, patch_rows, patch_cols, 3, half_patch, half_pa...]
    broadcast_in_dim x0 -> x4, local copies, waits for them, and re-layouts: none -> 2.3 us  [the longest x1 0.6 us: body(): gain_row = ln1_gain[None]]
    transpose x1, local copies, waits for them, and re-layouts: 0.99 us -> 3.13 us  [body(): cell_grads = cell_grads.reshape(planes, patch_rows, patch_cols, 3, half_p...]
    div x1 -> x0, matrix products: 1.97 us -> none  [attention(): return exp_scores / jnp.sum(exp_scores, axis=-1, keepdims=True)]
  transfers between devices with their start and end apart: 1 -> 1, of which waited for: 1 -> 1; matrix products, arithmetic and copies ran while one was open for 15% -> 18% of each run, Pallas kernels for 16% -> 18%
where the time goes in v2:
time: 140 us
  Pallas kernels  64.5 us (46%)
  local copies, waits for them, and re-layouts  37.5 us (27%)
  between operations  14.5 us (10%)
  other arithmetic  11.1 us (8%)
  waiting for transfers between devices  7.17 us (5%)
  matrix products  4.68 us (3%)
    pallas_call x5, Pallas kernels, exchange(): pl.pallas_call(functools.partial(exchange_kernel, axes, sizes, pick), out...  50.9 us
    pallas_call x2, Pallas kernels, local_call(): pl.pallas_call(kernel, out_shape=shapes, in_specs=[vmem] * len(operands),...  13.6 us
    all_gather x1, waiting for transfers between devices, body(): lax.all_gather(fill(weights_own, (feat_own, win.wide)), 'rows', axis=0, t...  7.16 us
    transpose x1, local copies, waits for them, and re-layouts, body(): patch_cells = picture.reshape(patch_rows, planes, 3, half_patch, patch_co...  3.29 us
    pad x5, local copies, waits for them, and re-layouts, fill(): jnp.pad(values, [(0, size - have) for size, have in zip(sizes, values.sha...  3.19 us
    transpose x1, local copies, waits for them, and re-layouts, body(): cell_grads = cell_grads.reshape(planes, patch_rows, patch_cols, 3, half_p...  3.13 us
    reduce_sum x3, other arithmetic, channel_group_sums(): per_col = jnp.sum(flat, axis=1).reshape(slab_imgs, col_count, chan_count)  3.05 us
    reshape x2, local copies, waits for them, and re-layouts, body(): dactive = dactive.reshape(slab_imgs, rows_here, flat_width)  2.83 us
  transfers between devices with their start and end apart: 1, of which 1 were waited for; matrix products, arithmetic and copies ran while one was open for 18% of the time, Pallas kernels for 18%

profile of v2, /device:TPU:0, one launch (start us, length us, event | category | flops | bytes accessed | tf_op | source)
XLA Modules:
  0.0 139.6 jit_solution(6081781842270866400)
XLA Ops:
  7.3 1.6 %convolution_convert_fusion.2 = bf16[147,320]{1,0:T(8,128)(2,1)S(1)} fusion(bf16[320,588]{1,0:T(8,128)(2,1)} %param.14, s32[588]{0:T(1024)S(1)} %fusion.64), kind=kOutput, calls=%fused_computation.7 | convolution fusion | flops 55538952 | bytes 472752 | tf_op jit(solution)/shard_map/dot_general | solution.py:345
  9.0 1.1 constant_dynamic-slice_fusion.1
  10.1 0.2 constant_dynamic-slice_fusion.2
  10.3 0.3 copy.56
  10.6 0.2 copy.57
  10.8 1.0 fusion.37
  11.8 0.4 fusion.3
  12.2 0.4 convert_reduce_fusion
  12.7 0.6 broadcast_in_dim.34.gain_ref
  13.3 0.6 broadcast_in_dim.35.final_ref
  13.9 0.6 broadcast_in_dim.36.head_w_ref
  14.6 0.1 reshape.327
  14.9 0.2 reshape.325
  15.3 0.6 pad.47.x_ref
  15.9 8.6 %shard_map.122 = f32[4,8,128]{2,1,0:T(8,128)} custom-call(f32[8,128]{1,0:T(8,128)} %pad.47.x_ref), custom_call_target="tpu_custom_call" | custom-call | tf_op jit(solution)/shard_map/pallas_call | solution.py:72
  24.5 0.7 reduce_sum.150
  25.6 0.1 tile.47
  25.8 0.1 tile.50
  25.9 0.3 fusion.13
  26.3 1.3 pad.70
  27.6 2.0 %reshape.330 = bf16[5016,64]{1,0:T(8,128)(2,1)S(1)} reshape(bf16[4,11,7296]{2,1,0:T(8,128)(2,1)} %pad.70) | data formatting | bytes 1284096 | tf_op jit(solution)/shard_map/reshape | solution.py:389
  29.6 1.4 %convolution_bitcast_fusion = f32[27,5016]{1,0:T(8,128)} fusion(bf16[5016,64]{1,0:T(8,128)(2,1)S(1)} %reshape.330, bf16[27,64]{1,0:T(8,128)(2,1)S(1)} %reshape.331), kind=kOutput, calls=%fused_computation | convolution fusion | flops 17335296 | bytes 1187232 | tf_op jit(solution)/shard_map/dot_general | solution.py:387
  31.1 2.3 %reshape.332 = f32[3,3,3,4,11,114]{5,4,3,2,1,0:T(8,128)S(1)} reshape(f32[27,5016]{1,0:T(8,128)} %convolution_bitcast_fusion) | data formatting | bytes 1083456 | tf_op jit(solution)/shard_map/reshape | solution.py:393
  33.4 0.2 fusion.43
  34.0 0.6 pad.50.x_ref
  34.6 16.5 %shard_map.123 = bf16[32,32,128]{2,1,0:T(8,128)(2,1)} custom-call(bf16[4,32,128]{2,1,0:T(8,128)(2,1)} %pad.50.x_ref), custom_call_target="tpu_custom_call" | custom-call | tf_op jit(solution)/shard_map/pallas_call | solution.py:72
  51.1 1.0 slice_convert_fusion
  52.1 0.3 copy.51
  52.4 0.7 reduce_sum.151
  53.2 1.5 %reshape.336 = bf16[4,4,3,7,16,7]{5,4,1,3,2,0:T(8,128)(2,1)S(1)} reshape(bf16[4,4,3,7,112]{4,1,3,2,0:T(4,128)(2,1)S(1)} %copy.52) | data formatting | bytes 150528 | tf_op jit(solution)/shard_map/reshape | solution.py:432
  54.7 3.3 %copy.53 = bf16[4,4,16,3,7,7]{2,1,0,5,4,3:T(4,128)(2,1)} copy(bf16[4,4,16,3,7,7]{5,2,0,4,3,1:T(8,128)(2,1)S(1)} %bitcast.115) | data formatting | bytes 150528 | tf_op jit(solution)/shard_map/transpose | solution.py:434
  58.0 1.6 %reshape.337 = bf16[256,147]{0,1:T(8,128)(2,1)S(1)} reshape(bf16[4,4,16,3,7,7]{2,1,0,5,4,3:T(4,128)(2,1)} %copy.53) | data formatting | bytes 150528 | tf_op jit(solution)/shard_map/reshape | solution.py:435
  59.8 0.7 pad.53.cells_ref
  60.5 0.8 and_convert_fusion.1.pick_out_ref
  61.2 1.2 and_convert_fusion.pick_qkv_ref
  62.4 7.2 %all-gather.2.cloned.1.call-done.w_ref = bf16[1280,896]{1,0:T(8,128)(2,1)} async-done(((bf16[320,896]{1,0:T(8,128)(2,1)}), bf16[1280,896]{1,0:T(8,128)(2,1)}) %all-gather.2.cloned.1.call-update) | async-done | bytes 2293776 | tf_op jit(solution)/shard_map/all_gather | solution.py:355
  69.5 5.6 %shard_map.124 = (f32[256,1280]{1,0:T(8,128)}, f32[256,128]{1,0:T(8,128)}, bf16[256,768]{1,0:T(8,128)(2,1)}, f32[256,128]{1,0:T(8,128)}, f32[4,1280]{1,0:T(4,128)}, /*index=5*/f32[4,1280]{1,0:T(4,128)}) custom-call(bf16[256,256]{1,0:T(8,128)(2,1)} %pad.53.cells_ref, bf16[1280,896]{1,0:T(8,128)(2,1)} %all-gather.2.cloned.1.call-done.w_ref, ...), custom_call_target="tpu_custom_call" | custom-call | tf_op jit(solution)/shard_map/pallas_call | solution.py:286
  75.2 7.0 %shard_map.125.mixed_ref = f32[8,4,1280]{2,1,0:T(4,128)} custom-call(f32[4,1280]{1,0:T(4,128)} %get-tuple-element.10.x_ref), custom_call_target="tpu_custom_call" | custom-call | tf_op jit(solution)/shard_map/pallas_call | solution.py:72
  82.2 0.5 broadcast_in_dim.37.first_ref
  82.7 8.0 %shard_map.126 = (bf16[256,256]{1,0:T(8,128)(2,1)}, f32[4,128]{1,0:T(4,128)}) custom-call(f32[8,4,1280]{2,1,0:T(4,128)} %shard_map.125.mixed_ref, f32[4,1280]{1,0:T(4,128)} %get-tuple-element.11.pooled_ref, f32[1,1280]{1,0:T(1,128)} %broadcast_in_dim.35.final_ref, f32[1,1280]{1,0:T(1,128)} %broadcast_in_dim.36.head_w_ref, ...), custom_call_target="tpu_custom_call" | custom-call | tf_op jit(solution)/shard_map/pallas_call | solution.py:286
  90.7 1.0 copy.58
  91.7 1.2 reshape.339
  92.9 3.1 %copy.59 = bf16[4,3,4,7,16,7]{5,4,0,3,2,1:T(8,128)(2,1)S(1)} copy(bf16[4,3,4,7,16,7]{4,2,0,5,3,1:T(4,128)(2,1)} %bitcast.125) | data formatting | bytes 150528 | tf_op jit(solution)/shard_map/transpose | solution.py:489
  96.0 1.4 reshape.340
  97.7 0.7 pad.56.x_ref
  98.4 10.1 %shard_map.127 = bf16[32,32,128]{2,1,0:T(8,128)(2,1)} custom-call(bf16[16,32,128]{2,1,0:T(8,128)(2,1)} %pad.56.x_ref), custom_call_target="tpu_custom_call" | custom-call | tf_op jit(solution)/shard_map/pallas_call | solution.py:72
  108.4 1.3 reshape.342
  109.8 0.1 reduce.1
  109.9 0.2 convolution_convert_fusion
  110.9 1.0 reshape.345
  111.9 1.3 fusion.85
  113.2 1.4 %reshape.346 = f32[4,7,1,7168]{3,1,0,2:T(8,128)} reshape(f32[3136,64]{1,0:T(8,128)S(1)} %fusion.85) | data formatting | bytes 1605632 | tf_op jit(solution)/shard_map/reshape | solution.py:524
  114.6 1.4 %reshape.347 = f32[4,7,7168]{2,1,0:T(8,128)} reshape(f32[3136,64]{1,0:T(8,128)S(1)} %fusion.85) | data formatting | bytes 1605632 | tf_op jit(solution)/shard_map/reshape | solution.py:524
  116.1 2.2 %fusion.83 = (f32[4,7168]{1,0:T(4,128)S(1)}, f32[4,7168]{1,0:T(4,128)S(1)}) fusion(f32[4,7168]{1,0:T(4,128)S(1)} %tile.47, f32[4,7168]{1,0:T(4,128)S(1)} %tile.50, bf16[4,7,1,7168]{3,0,2,1:T(4,128)(2,1)S(1)} %copy-done.1, f32[4,7,7168]{2,1,0:T(8,128)} %reshape.347, f32[7168]{0:T(1024)S(1)} %mul.132), kind=kLoop, calls=%fused_computation.157 | loop fusion | flops 3153920 | bytes 1691648 | tf_op jit(solution)/shard_map/reduce_sum | solution.py:360
  118.3 0.1 reshape.348
  118.7 0.2 reshape.350
  119.1 0.6 pad.58.x_ref
  119.7 8.7 %shard_map.128 = f32[4,8,128]{2,1,0:T(8,128)} custom-call(f32[8,128]{1,0:T(8,128)} %pad.58.x_ref), custom_call_target="tpu_custom_call" | custom-call | tf_op jit(solution)/shard_map/pallas_call | solution.py:72
  128.4 0.7 reduce_sum.159
  129.5 0.1 tile.57
  129.7 0.1 tile.54
  129.8 0.6 fusion.34
  130.5 1.1 copy.65
  131.5 1.2 constant_dynamic-slice_fusion
  (81 shorter events, 3.5 us)
Async XLA Ops:
  7.2 2.9 %copy-start = (bf16[320,3,640]{2,0,1:T(8,128)(2,1)S(1)}, bf16[320,3,640]{2,0,1:T(8,128)(2,1)}, u32[]{:S(2)}) copy-start(bf16[320,3,640]{2,0,1:T(8,128)(2,1)} %param.17) | copy-start | bytes 3686404
  7.2 62.4 %all-gather.2.cloned.1.call-start = ((), (), s32[]{:S(2)}) async-start(), calls=%async_computation | async-start | bytes 2867200 | tf_op jit(solution)/shard_map/all_gather | solution.py:355
  10.6 1.2 copy-start.1
  10.8 1.9 %copy-start.4 = (f32[1280]{0:T(1024)S(1)}, f32[1280]{0:T(1024)}, u32[]{:S(2)}) copy-start(f32[1280]{0:T(1024)} %param.16) | copy-start | bytes 15364
  10.8 2.5 %copy-start.5 = (f32[1280]{0:T(1024)S(1)}, f32[1280]{0:T(1024)}, u32[]{:S(2)}) copy-start(f32[1280]{0:T(1024)} %param.19) | copy-start | bytes 15364
  10.8 3.0 %copy-start.6 = (f32[1280]{0:T(1024)S(1)}, f32[1280]{0:T(1024)}, u32[]{:S(2)}) copy-start(f32[1280]{0:T(1024)} %param.20) | copy-start | bytes 15364
  10.8 3.6 %copy-start.3 = (bf16[3,3,3,64]{3,2,1,0:T(4,128)(2,1)S(1)}, bf16[3,3,3,64]{3,2,1,0:T(4,128)(2,1)}, u32[]{:S(2)}) copy-start(bf16[3,3,3,64]{3,2,1,0:T(4,128)(2,1)} %param.13) | copy-start | bytes 10372
  10.8 3.6 %copy-start.8 = (f32[64]{0:T(128)S(1)}, f32[64]{0:T(128)}, u32[]{:S(2)}) copy-start(f32[64]{0:T(128)} %param.12) | copy-start | bytes 772
  31.1 2.7 %copy-start.7 = (s32[1,4]{1,0:T(1,128)S(1)}, s32[1,4]{1,0:T(1,128)}, u32[]{:S(2)}) copy-start(s32[1,4]{1,0:T(1,128)} %param.21) | copy-start | bytes 52
  118.3 11.5 %copy-start.2 = (f32[4,7,1,7168]{3,1,0,2:T(8,128)S(1)}, f32[4,7,1,7168]{3,1,0,2:T(8,128)}, u32[]{:S(2)}) copy-start(f32[4,7,1,7168]{3,1,0,2:T(8,128)} %reshape.346) | copy-start | bytes 2408452
Sparse Core Ops, SparseCore 0:
  11.9 57.5 all-gather.1

commit v3 on v2

--- a/solution.py
+++ b/solution.py
@@ -144,6 +144,19 @@
         return hit.astype(jnp.bfloat16)
 
 
+def cell_masks(rows_of, patch_cols, half_patch, fold):
+    columns = patch_cols * half_patch
+    place = lax.broadcasted_iota(jnp.int32, (rows_of, patch_cols, 128), 1) * half_patch
+    lane = lax.broadcasted_iota(jnp.int32, (rows_of, patch_cols, 128), 2)
+    inside = ((lane >= place) & (lane < place + half_patch)).astype(jnp.float32)
+    pixel = lax.broadcasted_iota(jnp.int32, (128, fold), 0)
+    offset = lax.broadcasted_iota(jnp.int32, (128, fold), 1) - pixel
+    for patch in range(1, patch_cols):
+        offset = offset + jnp.where(pixel >= patch * half_patch, half_patch, 0)
+    offset = jnp.where(pixel < columns, offset, -1)
+    return inside.reshape(rows_of * patch_cols, 128), offset
+
+
 def over(count, step):
     if count == 1:
         step(0)
@@ -155,16 +168,27 @@
 
 
 def scorer_forward(
-    win, planes, tokens, per_chunk, cells_ref, w_ref, pick_qkv_ref, pick_out_ref, pos_ref, gain_ref,
+    win, planes, tokens, per_chunk, half_patch, patch_cols, pics_ref, w_ref, pick_qkv_ref, pick_out_ref, pos_ref, gain_ref,
     hat_ref, inv_ref, heads_ref, prob_ref, mixed_ref, pooled_ref, att_ref,
 ):
     heads = win.heads
     rows = per_chunk * tokens
+    rows_of = rows // patch_cols
+    inside, offset = cell_masks(rows_of, patch_cols, half_patch, win.fold)
     factor = 1.0 / math.sqrt(HEAD_DIM)
 
     def embed(index):
         at = pl.ds(pl.multiple_of(index * rows, rows), rows)
-        embedded = mm(cells_ref[at, :], w_ref[:, : win.fold], 1, 1)
+        cells = jnp.zeros((rows, win.fold), jnp.float32)
+        lines = pl.ds(pl.multiple_of(index * rows_of, rows_of), rows_of)
+        for line in range(pics_ref.shape[0]):
+            spread = jnp.broadcast_to(
+                pics_ref[line, lines, :][:, None, :], (rows_of, patch_cols, 128)
+            ).reshape(rows, 128)
+            cells = cells + mm(
+                hold(spread * inside), hold((offset == line * half_patch).astype(jnp.float32)), 1, 0
+            )
+        embedded = mm(hold(cells), w_ref[:, : win.fold], 1, 1)
         width = embedded.shape[1]
         embedded = embedded.reshape(per_chunk, tokens, width) + pos_ref[...].astype(jnp.float32)[None]
         for inner in range(per_chunk):
@@ -214,12 +238,14 @@
 
 
 def scorer_backward(
-    win, planes, tokens, per_chunk, mixed_ref, pooled_ref, final_ref, head_w_ref, first_ref, w_ref,
+    win, planes, tokens, per_chunk, half_patch, patch_cols, mixed_ref, pooled_ref, final_ref, head_w_ref, first_ref, w_ref,
     pick_qkv_ref, pick_out_ref, gain_ref, hat_ref, inv_ref, heads_ref, prob_ref,
-    dcells_ref, reward_ref, grad_ref, up_ref, share_ref,
+    dpics_ref, reward_ref, grad_ref, up_ref, share_ref,
 ):
     heads = win.heads
     rows = per_chunk * tokens
+    rows_of = rows // patch_cols
+    inside, offset = cell_masks(rows_of, patch_cols, half_patch, win.fold)
     factor = 1.0 / math.sqrt(HEAD_DIM)
     pooled = pooled_ref[...]
     for index in range(mixed_ref.shape[0]):
@@ -276,7 +302,13 @@
             for inner in range(per_chunk)
         ]
         dembedded = hold(jnp.concatenate(pieces, axis=0) if per_chunk > 1 else pieces[0])
-        dcells_ref[at, :] = hold(mm(dembedded, w_ref[:, : win.fold], 1, 0))
+        dcells = hold(mm(dembedded, w_ref[:, : win.fold], 1, 0))
+        lines = pl.ds(pl.multiple_of(index * rows_of, rows_of), rows_of)
+        for line in range(dpics_ref.shape[0]):
+            spread = inside * mm(
+                dcells, hold((offset == line * half_patch).astype(jnp.float32)), 1, 1
+            )
+            dpics_ref[line, lines, :] = jnp.sum(spread.reshape(rows_of, patch_cols, 128), axis=1)
 
     over(planes // per_chunk, finish)
 
@@ -421,24 +453,24 @@
         planes * tp_devices,
         2,
     )
-    slabs = slabs[:, :rim_entries, :col_count].astype(jnp.float32)
-    slabs = slabs.reshape(row_devices, planes, tp_devices, 3, out_rows, col_count)
+    slabs = slabs[:, :rim_entries].astype(jnp.float32)
+    slabs = slabs.reshape(row_devices, planes, tp_devices, 3, out_rows, 128)
     slabs = jnp.sum(slabs, axis=2)
     middle = slabs[:, :, :, 1:-1]
     above = jnp.pad(slabs[:-1, :, :, -1:], ((1, 0), (0, 0), (0, 0), (0, rows_here - 1), (0, 0)))
     below = jnp.pad(slabs[1:, :, :, :1], ((0, 1), (0, 0), (0, 0), (rows_here - 1, 0), (0, 0)))
-    picture = (middle + above + below).astype(jnp.bfloat16)
-
-    patch_cells = picture.reshape(
-        patch_rows, planes, 3, half_patch, patch_cols, half_patch
-    ).transpose(1, 0, 4, 2, 3, 5)
-    patch_cells = patch_cells.reshape(planes * tokens, cell_entries)
+    picture = (middle + above + below).astype(jnp.bfloat16).astype(jnp.float32)
+    picture_lines = picture.transpose(2, 3, 1, 0, 4).reshape(
+        3 * half_patch, planes * patch_rows, 128
+    )
     total_rows = planes * tokens
     per_chunk = max(1, min(planes, 256 // tokens))
     shape = jax.ShapeDtypeStruct
     gain_row = ln1_gain[None]
     hat_in, inv_in, head_cols, prob_soft, mixed, pooled_in = local_call(
-        functools.partial(scorer_forward, win, planes, tokens, per_chunk),
+        functools.partial(
+            scorer_forward, win, planes, tokens, per_chunk, half_patch, patch_cols
+        ),
         [
             shape((total_rows, width), jnp.float32),
             shape((total_rows, 128), jnp.float32),
@@ -448,7 +480,7 @@
             shape((planes, width), jnp.float32),
         ],
         [pltpu.VMEM((planes, heads_mine * 128), jnp.float32)],
-        fill(patch_cells, (total_rows, win.fold)),
+        picture_lines,
         weights,
         pick_qkv,
         pick_out,
@@ -458,9 +490,11 @@
     mixed = exchange(mixed, split_axes + ("tp",), None, 3)
     first = jnp.where(plane_index + lax.axis_index("tp") == 0, 1.0, 0.0)
     cell_grads, rewards = local_call(
-        functools.partial(scorer_backward, win, planes, tokens, per_chunk),
+        functools.partial(
+            scorer_backward, win, planes, tokens, per_chunk, half_patch, patch_cols
+        ),
         [
-            shape((total_rows, win.fold), jnp.bfloat16),
+            shape((3 * half_patch, planes * patch_rows, 128), jnp.float32),
             shape((planes, 128), jnp.float32),
         ],
         [
@@ -483,16 +517,14 @@
         prob_soft,
     )
     rewards = lax.dynamic_slice_in_dim(rewards[:, 0], plane_index, 1)
-    cell_grads = cell_grads[:, :cell_entries]
-    cell_grads = cell_grads.reshape(
-        planes, patch_rows, patch_cols, 3, half_patch, half_patch
-    ).transpose(0, 3, 1, 4, 2, 5)
+    cell_grads = cell_grads.astype(jnp.bfloat16).reshape(3, half_patch, planes, patch_rows, 128)
     back_image = jnp.pad(
-        cell_grads.reshape(planes, 3, rows_total, col_count), ((0, 0), (0, 0), (1, 1), (0, 0))
+        cell_grads.transpose(2, 0, 3, 1, 4).reshape(planes, 3, rows_total, 128),
+        ((0, 0), (0, 0), (1, 1), (0, 0)),
     )
     slabs_back = jnp.stack(
         [back_image[:, :, r * rows_here : r * rows_here + out_rows] for r in range(row_devices)]
-    ).reshape(row_devices * planes, rim_entries, col_count)
+    ).reshape(row_devices * planes, rim_entries, 128)
     returned = exchange(
         fill(slabs_back, (row_devices * planes, up16(rim_entries), 128)),
         ("rows",) + split_axes + ("tp",),

time: 140 us -> 137 us (0.979)
  local copies, waits for them, and re-layouts: 37.5 us -> 24.3 us
  waiting for transfers between devices: 7.17 us -> 13.8 us
  Pallas kernels: 64.5 us -> 67.1 us
    all_gather x1, waiting for transfers between devices: 7.16 us -> 13.8 us  [body(): lax.all_gather(fill(weights_own, (feat_own, win.wide)), 'rows', axis=0, t...]
    transpose x2 -> x0, local copies, waits for them, and re-layouts: 6.42 us -> none  [the longest x1 3.29 us: body(): patch_cells = picture.reshape(patch_rows, planes, 3, half_patch, patch_co...]
    reshape x6 -> x3, local copies, waits for them, and re-layouts: 6.11 us -> 1.03 us  [the longest x1 0.73 us: body(): picture.transpose(2, 3, 1, 0, 4)]
    pallas_call x2, Pallas kernels: 13.6 us -> 16.2 us  [local_call(): pl.pallas_call(kernel, out_shape=shapes, in_specs=[vmem] * len(operands),...]
    pad x5 -> x4, local copies, waits for them, and re-layouts: 3.19 us -> 2.52 us  [fill(): jnp.pad(values, [(0, size - have) for size, have in zip(sizes, values.sha...]
  transfers between devices with their start and end apart: 1 -> 1, of which waited for: 1 -> 1; matrix products, arithmetic and copies ran while one was open for 18% -> 14% of each run, Pallas kernels for 18% -> 18%
where the time goes in v3:
time: 137 us; the launch traced here: 136 us
  Pallas kernels  67.1 us (49%)
  local copies, waits for them, and re-layouts  24.3 us (18%)
  between operations  14.5 us (11%)
  waiting for transfers between devices  13.8 us (10%)
  other arithmetic  12 us (9%)
  matrix products  4.66 us (3%)
    pallas_call x5, Pallas kernels, exchange(): pl.pallas_call(functools.partial(exchange_kernel, axes, sizes, pick), out...  50.9 us
    pallas_call x2, Pallas kernels, local_call(): pl.pallas_call(kernel, out_shape=shapes, in_specs=[vmem] * len(operands),...  16.2 us
    all_gather x1, waiting for transfers between devices, body(): lax.all_gather(fill(weights_own, (feat_own, win.wide)), 'rows', axis=0, t...  13.8 us
    reduce_sum x3, other arithmetic, channel_group_sums(): per_col = jnp.sum(flat, axis=1).reshape(slab_imgs, col_count, chan_count)  3.05 us
    reshape x2, local copies, waits for them, and re-layouts, body(): dactive = dactive.reshape(slab_imgs, rows_here, flat_width)  2.83 us
  transfers between devices with their start and end apart: 1, of which 1 were waited for; matrix products, arithmetic and copies ran while one was open for 14% of the time, Pallas kernels for 18%

profile of v3, /device:TPU:0, one launch (start us, length us, event | category | flops | bytes accessed | tf_op | source)
XLA Modules:
  0.0 136.4 jit_solution(3045387506205793919)
XLA Ops:
  7.3 1.6 %convolution_convert_fusion.2 = bf16[147,320]{1,0:T(8,128)(2,1)S(1)} fusion(bf16[320,588]{1,0:T(8,128)(2,1)} %param.14, s32[588]{0:T(1024)S(1)} %fusion.64), kind=kOutput, calls=%fused_computation.7 | convolution fusion | flops 55538952 | bytes 472752 | tf_op jit(solution)/shard_map/dot_general | solution.py:377
  8.9 0.1 copy.47
  9.0 1.1 constant_dynamic-slice_fusion.1
  10.1 0.2 constant_dynamic-slice_fusion.2
  10.3 0.3 copy.48
  10.6 0.2 copy.49
  10.8 0.9 fusion.37
  11.8 0.4 fusion.3
  12.2 0.4 convert_reduce_fusion
  12.6 0.6 broadcast_in_dim.34.gain_ref
  13.2 0.6 broadcast_in_dim.35.final_ref
  13.8 0.6 broadcast_in_dim.36.head_w_ref
  14.5 0.1 reshape.326
  14.9 0.2 reshape.324
  15.3 0.6 pad.43.x_ref
  15.9 8.6 %shard_map.122 = f32[4,8,128]{2,1,0:T(8,128)} custom-call(f32[8,128]{1,0:T(8,128)} %pad.43.x_ref), custom_call_target="tpu_custom_call" | custom-call | tf_op jit(solution)/shard_map/pallas_call | solution.py:72
  24.5 0.7 reduce_sum.150
  25.6 0.1 tile.47
  25.8 0.1 tile.50
  25.9 0.3 fusion.13
  26.3 1.4 pad.65
  27.6 2.0 %reshape.329 = bf16[5016,64]{1,0:T(8,128)(2,1)S(1)} reshape(bf16[4,11,7296]{2,1,0:T(8,128)(2,1)} %pad.65) | data formatting | bytes 1284096 | tf_op jit(solution)/shard_map/reshape | solution.py:421
  29.6 1.4 %convolution_bitcast_fusion = f32[27,5016]{1,0:T(8,128)} fusion(bf16[5016,64]{1,0:T(8,128)(2,1)S(1)} %reshape.329, bf16[27,64]{1,0:T(8,128)(2,1)S(1)} %reshape.330), kind=kOutput, calls=%fused_computation | convolution fusion | flops 17335296 | bytes 1187232 | tf_op jit(solution)/shard_map/dot_general | solution.py:419
  31.0 2.3 %reshape.331 = f32[3,3,3,4,11,114]{5,4,3,2,1,0:T(8,128)S(1)} reshape(f32[27,5016]{1,0:T(8,128)} %convolution_bitcast_fusion) | data formatting | bytes 1083456 | tf_op jit(solution)/shard_map/reshape | solution.py:425
  33.4 0.2 fusion.43
  33.6 0.1 convert_element_type.85
  33.7 0.1 convolution_convert_fusion.1
  33.9 0.1 reshape.332
  34.0 0.6 pad.46.x_ref
  34.6 16.5 %shard_map.123 = bf16[32,32,128]{2,1,0:T(8,128)(2,1)} custom-call(bf16[4,32,128]{2,1,0:T(8,128)(2,1)} %pad.46.x_ref), custom_call_target="tpu_custom_call" | custom-call | tf_op jit(solution)/shard_map/pallas_call | solution.py:72
  51.1 1.0 slice_convert_fusion
  52.1 0.3 copy.45
  52.4 0.6 reduce_sum.151
  53.0 0.7 copy.46
  53.8 0.8 and_convert_fusion.1.pick_out_ref
  54.6 1.2 and_convert_fusion.pick_qkv_ref
  55.8 13.8 %all-gather.2.cloned.1.call-done.w_ref = bf16[1280,896]{1,0:T(8,128)(2,1)} async-done(((bf16[320,896]{1,0:T(8,128)(2,1)}), bf16[1280,896]{1,0:T(8,128)(2,1)}) %all-gather.2.cloned.1.call-update) | async-done | bytes 2293776 | tf_op jit(solution)/shard_map/all_gather | solution.py:387
  69.5 7.3 %shard_map.124 = (f32[256,1280]{1,0:T(8,128)}, f32[256,128]{1,0:T(8,128)}, bf16[256,768]{1,0:T(8,128)(2,1)}, f32[256,128]{1,0:T(8,128)}, f32[4,1280]{1,0:T(4,128)}, /*index=5*/f32[4,1280]{1,0:T(4,128)}) custom-call(f32[21,16,128]{2,1,0:T(8,128)} %bitcast.121, bf16[1280,896]{1,0:T(8,128)(2,1)} %all-gather.2.cloned.1.call-done.w_ref, ...), custom_call_target="tpu_custom_call" | custom-call | tf_op jit(solution)/shard_map/pallas_call | solution.py:318
  76.8 7.0 %shard_map.125.mixed_ref = f32[8,4,1280]{2,1,0:T(4,128)} custom-call(f32[4,1280]{1,0:T(4,128)} %get-tuple-element.10.x_ref), custom_call_target="tpu_custom_call" | custom-call | tf_op jit(solution)/shard_map/pallas_call | solution.py:72
  83.9 0.5 broadcast_in_dim.37.first_ref
  84.4 8.9 %shard_map.126 = (f32[21,16,128]{2,1,0:T(8,128)}, f32[4,128]{1,0:T(4,128)}) custom-call(f32[8,4,1280]{2,1,0:T(4,128)} %shard_map.125.mixed_ref, f32[4,1280]{1,0:T(4,128)} %get-tuple-element.11.pooled_ref, f32[1,1280]{1,0:T(1,128)} %broadcast_in_dim.35.final_ref, f32[1,1280]{1,0:T(1,128)} %broadcast_in_dim.36.head_w_ref, ...), custom_call_target="tpu_custom_call" | custom-call | tf_op jit(solution)/shard_map/pallas_call | solution.py:318
  93.3 0.9 convert_element_type.92
  94.5 0.7 pad.51.x_ref
  95.2 10.1 %shard_map.127 = bf16[32,32,128]{2,1,0:T(8,128)(2,1)} custom-call(bf16[16,32,128]{2,1,0:T(8,128)(2,1)} %pad.51.x_ref), custom_call_target="tpu_custom_call" | custom-call | tf_op jit(solution)/shard_map/pallas_call | solution.py:72
  105.2 1.3 reshape.341
  106.5 0.1 reduce.1
  106.7 0.2 convolution_convert_fusion
  106.9 0.1 reshape.343
  107.1 0.1 bitcast_dynamic-update-slice_fusion.4
  107.7 1.0 reshape.344
  108.7 1.3 fusion.85
  110.0 1.4 %reshape.345 = f32[4,7,1,7168]{3,1,0,2:T(8,128)} reshape(f32[3136,64]{1,0:T(8,128)S(1)} %fusion.85) | data formatting | bytes 1605632 | tf_op jit(solution)/shard_map/reshape | solution.py:556
  111.4 1.4 %reshape.346 = f32[4,7,7168]{2,1,0:T(8,128)} reshape(f32[3136,64]{1,0:T(8,128)S(1)} %fusion.85) | data formatting | bytes 1605632 | tf_op jit(solution)/shard_map/reshape | solution.py:556
  112.9 2.2 %fusion.83 = (f32[4,7168]{1,0:T(4,128)S(1)}, f32[4,7168]{1,0:T(4,128)S(1)}) fusion(f32[4,7168]{1,0:T(4,128)S(1)} %tile.47, f32[4,7168]{1,0:T(4,128)S(1)} %tile.50, bf16[4,7,1,7168]{3,0,2,1:T(4,128)(2,1)S(1)} %copy-done.1, f32[4,7,7168]{2,1,0:T(8,128)} %reshape.346, f32[7168]{0:T(1024)S(1)} %mul.132), kind=kLoop, calls=%fused_computation.158 | loop fusion | flops 3153920 | bytes 1691648 | tf_op jit(solution)/shard_map/reduce_sum | solution.py:392
  115.1 0.1 reshape.347
  115.5 0.2 reshape.349
  115.9 0.6 pad.53.x_ref
  116.5 8.7 %shard_map.128 = f32[4,8,128]{2,1,0:T(8,128)} custom-call(f32[8,128]{1,0:T(8,128)} %pad.53.x_ref), custom_call_target="tpu_custom_call" | custom-call | tf_op jit(solution)/shard_map/pallas_call | solution.py:72
  125.2 0.7 reduce_sum.159
  126.3 0.1 tile.57
  126.5 0.1 tile.54
  126.6 0.6 fusion.34
  127.2 1.1 copy.56
  128.3 1.2 constant_dynamic-slice_fusion
  (74 shorter events, 2.7 us)
Async XLA Ops:
  7.2 2.9 %copy-start = (bf16[320,3,640]{2,0,1:T(8,128)(2,1)S(1)}, bf16[320,3,640]{2,0,1:T(8,128)(2,1)}, u32[]{:S(2)}) copy-start(bf16[320,3,640]{2,0,1:T(8,128)(2,1)} %param.17) | copy-start | bytes 3686404
  7.2 62.4 %all-gather.2.cloned.1.call-start = ((), (), s32[]{:S(2)}) async-start(), calls=%async_computation | async-start | bytes 2867200 | tf_op jit(solution)/shard_map/all_gather | solution.py:387
  10.6 1.2 copy-start.1
  10.8 1.9 %copy-start.4 = (f32[1280]{0:T(1024)S(1)}, f32[1280]{0:T(1024)}, u32[]{:S(2)}) copy-start(f32[1280]{0:T(1024)} %param.16) | copy-start | bytes 15364
  10.8 2.4 %copy-start.5 = (f32[1280]{0:T(1024)S(1)}, f32[1280]{0:T(1024)}, u32[]{:S(2)}) copy-start(f32[1280]{0:T(1024)} %param.19) | copy-start | bytes 15364
  10.8 3.0 %copy-start.6 = (f32[1280]{0:T(1024)S(1)}, f32[1280]{0:T(1024)}, u32[]{:S(2)}) copy-start(f32[1280]{0:T(1024)} %param.20) | copy-start | bytes 15364
  10.8 3.6 %copy-start.3 = (bf16[3,3,3,64]{3,2,1,0:T(4,128)(2,1)S(1)}, bf16[3,3,3,64]{3,2,1,0:T(4,128)(2,1)}, u32[]{:S(2)}) copy-start(bf16[3,3,3,64]{3,2,1,0:T(4,128)(2,1)} %param.13) | copy-start | bytes 10372
  10.8 3.6 %copy-start.8 = (f32[64]{0:T(128)S(1)}, f32[64]{0:T(128)}, u32[]{:S(2)}) copy-start(f32[64]{0:T(128)} %param.12) | copy-start | bytes 772
  31.0 2.7 %copy-start.7 = (s32[1,4]{1,0:T(1,128)S(1)}, s32[1,4]{1,0:T(1,128)}, u32[]{:S(2)}) copy-start(s32[1,4]{1,0:T(1,128)} %param.21) | copy-start | bytes 52
  115.1 11.5 %copy-start.2 = (f32[4,7,1,7168]{3,1,0,2:T(8,128)S(1)}, f32[4,7,1,7168]{3,1,0,2:T(8,128)}, u32[]{:S(2)}) copy-start(f32[4,7,1,7168]{3,1,0,2:T(8,128)} %reshape.345) | copy-start | bytes 2408452
Sparse Core Ops, SparseCore 0:
  11.9 57.5 all-gather.1
